TPU v7x, 32 devices: a whole 2x2x4 slice. The times are simulated.
32 devices in a mesh: row: 8 (over z, y), col: 4 (over x, core).
Axes of the slice: x: 2, y: 2, z: 4, core: 2. Of those that a mesh axis runs over, the one named last changes fastest.
Arguments:
- signal: bfloat16 [8, 256, 512], P(None, 'row', 'col'), may hold values from -6 to 6
- filter_real: bfloat16 [8, 256, 512], P(None, 'row', 'col'), may hold values from -6 to 6
- filter_imag: bfloat16 [8, 256, 512], P(None, 'row', 'col'), may hold values from -6 to 6
- skip: float32 [8], replicated, may hold values from 0.5 to 1.5
Outputs:
- output: bfloat16 [8, 256, 512], P(None, 'row', 'col')
All inputs are finite; a program needn't handle non-finite values.
Results may differ from a plain program's by a relative error of at most 0.0064.
Values may be sent and summed in bfloat16 or wider, within the bound.
No kernel may reach another device: no remote copies, remote signals or barrier semaphores. Data moves between devices by JAX's collectives and lax.ppermute only.
A program may use at most 64 MiB of HBM per device.

v0:
```python
import math

import jax
import jax.numpy as jnp
from jax import lax
from jax.sharding import PartitionSpec as P


def phase_table(left_ids, right_ids, modulus):
    product = left_ids[:, None] * right_ids[None, :] % modulus
    angle = -2.0 * math.pi / modulus * product.astype(jnp.float32)
    return (jnp.cos(angle).astype(jnp.bfloat16), jnp.sin(angle).astype(jnp.bfloat16))


def twist_table(left_ids, right_ids, modulus):
    product = left_ids[:, None] * right_ids[None, :] % modulus
    angle = -2.0 * math.pi / modulus * product.astype(jnp.float32)
    return (jnp.cos(angle), jnp.sin(angle))


def column_product(series, phase):
    return jnp.einsum("crn,nk->crk", series, phase, preferred_element_type=jnp.float32)


def row_product(phase, series):
    return jnp.einsum("rn,cnj->crj", phase, series, preferred_element_type=jnp.float32)


def local(signal, filter_real, filter_imag, skip):
    channels, row_count, col_count = signal.shape
    first_len = row_count * lax.axis_size("row")
    second_len = col_count * lax.axis_size("col")
    seq_len = first_len * second_len
    row_offset = lax.axis_index("row") * row_count
    col_offset = lax.axis_index("col") * col_count
    own_rows = row_offset + jnp.arange(row_count, dtype=jnp.int32)
    own_cols = col_offset + jnp.arange(col_count, dtype=jnp.int32)
    twist_re, twist_im = twist_table(own_rows, own_cols, seq_len)
    pair_width = col_count // lax.axis_size("row")
    pair_cols = (
        col_offset + lax.axis_index("row") * pair_width + jnp.arange(pair_width, dtype=jnp.int32)
    )
    all_rows = jnp.arange(first_len, dtype=jnp.int32)
    full_re, full_im = phase_table(all_rows, all_rows, first_len)
    columns_whole = lax.all_to_all(signal, "row", split_axis=2, concat_axis=1, tiled=True)
    pair_b_re = row_product(full_re, columns_whole)
    pair_b_im = row_product(full_im, columns_whole)
    pair_tw_re, pair_tw_im = twist_table(all_rows, pair_cols, seq_len)
    pair_mix_re = (pair_b_re * pair_tw_re - pair_b_im * pair_tw_im).astype(jnp.bfloat16)
    pair_mix_im = (pair_b_re * pair_tw_im + pair_b_im * pair_tw_re).astype(jnp.bfloat16)
    mixed_re, mixed_im = (
        lax.all_to_all(pair_mix_re, "row", split_axis=1, concat_axis=2, tiled=True),
        lax.all_to_all(pair_mix_im, "row", split_axis=1, concat_axis=2, tiled=True),
    )
    pieces = (
        lax.all_gather(mixed_re, "col", axis=2, tiled=True),
        lax.all_gather(mixed_im, "col", axis=2, tiled=True),
    )
    amount = pieces[0].shape[2]
    phase_re, phase_im = phase_table(jnp.arange(amount, dtype=jnp.int32), own_cols, second_len)
    part_re, part_im = pieces
    new_re = column_product(part_re, phase_re) - column_product(part_im, phase_im)
    new_im = column_product(part_re, phase_im) + column_product(part_im, phase_re)
    spec_re = new_re
    spec_im = new_im
    prod_re = (spec_re * filter_real - spec_im * filter_imag).astype(jnp.bfloat16)
    prod_im = (spec_re * filter_imag + spec_im * filter_real).astype(jnp.bfloat16)
    pieces = (
        lax.all_gather(prod_re, "col", axis=2, tiled=True),
        lax.all_gather(prod_im, "col", axis=2, tiled=True),
    )
    amount = pieces[0].shape[2]
    phase_re, phase_im = phase_table(jnp.arange(amount, dtype=jnp.int32), own_cols, second_len)
    part_re, part_im = pieces
    new_re = column_product(part_re, phase_re) + column_product(part_im, phase_im)
    new_im = column_product(part_im, phase_re) - column_product(part_re, phase_im)
    unwound_re = (new_re * twist_re + new_im * twist_im).astype(jnp.bfloat16)
    unwound_im = (new_im * twist_re - new_re * twist_im).astype(jnp.bfloat16)
    pair_un_re, pair_un_im = (
        lax.all_to_all(unwound_re, "row", split_axis=2, concat_axis=1, tiled=True),
        lax.all_to_all(unwound_im, "row", split_axis=2, concat_axis=1, tiled=True),
    )
    pair_total = row_product(full_re, pair_un_re) + row_product(full_im, pair_un_im)
    pair_out = (
        pair_total / seq_len + skip[:, None, None] * columns_whole.astype(jnp.float32)
    ).astype(jnp.bfloat16)
    return lax.all_to_all(pair_out, "row", split_axis=1, concat_axis=2, tiled=True)


def solution(mesh):
    in_specs = (P(None, "row", "col"), P(None, "row", "col"), P(None, "row", "col"), P())
    out_specs = P(None, "row", "col")
    return jax.shard_map(local, mesh=mesh, in_specs=in_specs, out_specs=out_specs, check_vma=False)
```

profile of v0, /device:TPU:0, one launch (start us, length us, event | category | flops | bytes accessed | tf_op | source)
XLA Modules:
  0.0 107.6 jit_solution(13827530816031073000)
XLA Ops:
  1.9 7.3 %all-to-all-start = ((bf16[8,2,2048]{2,1,0:T(2,128)(2,1)}), bf16[8,2,2048]{2,1,0:T(2,128)(2,1)S(1)}, u32[]{:S(2)}, u32[]{:S(2)}) async-start(bf16[8,2,2048]{2,1,0:T(2,128)(2,1)} %reshape.142), calls=%async_computation | async-start | bytes 131072 | tf_op jit(solution)/shard_map/all_to_all | solution.py:45
  9.4 6.7 %all-to-all-done = bf16[8,2,2048]{2,1,0:T(2,128)(2,1)S(1)} async-done(((bf16[8,2,2048]{2,1,0:T(2,128)(2,1)}), bf16[8,2,2048]{2,1,0:T(2,128)(2,1)S(1)}, u32[]{:S(2)}, u32[]{:S(2)}) %all-to-all-start) | async-done | bytes 65568 | tf_op jit(solution)/shard_map/all_to_all | solution.py:45
  19.3 1.2 %reshape.144 = bf16[8,2,2048]{2,1,0:T(2,128)(2,1)} reshape(bf16[256,8,16]{2,1,0:T(8,128)(2,1)S(1)} %bitcast.96) | data formatting | bytes 131072
  20.5 3.4 %all-to-all-start.1 = ((bf16[8,2,2048]{2,1,0:T(2,128)(2,1)}), bf16[8,2,2048]{2,1,0:T(2,128)(2,1)S(1)}, u32[]{:S(2)}, u32[]{:S(2)}) async-start(bf16[8,2,2048]{2,1,0:T(2,128)(2,1)} %reshape.144), calls=%async_computation.1 | async-start | bytes 131072 | tf_op jit(solution)/shard_map/all_to_all | solution.py:52
  24.3 1.2 %reshape.146 = bf16[8,2,2048]{2,1,0:T(2,128)(2,1)} reshape(bf16[256,8,16]{2,1,0:T(8,128)(2,1)S(1)} %bitcast.97) | data formatting | bytes 131072
  25.5 5.2 %all-to-all-done.1 = bf16[8,2,2048]{2,1,0:T(2,128)(2,1)S(1)} async-done(((bf16[8,2,2048]{2,1,0:T(2,128)(2,1)}), bf16[8,2,2048]{2,1,0:T(2,128)(2,1)S(1)}, u32[]{:S(2)}, u32[]{:S(2)}) %all-to-all-start.1) | async-done | bytes 65568 | tf_op jit(solution)/shard_map/all_to_all | solution.py:52
  30.7 3.3 %all-to-all-start.2 = ((bf16[8,2,2048]{2,1,0:T(2,128)(2,1)}), bf16[8,2,2048]{2,1,0:T(2,128)(2,1)S(1)}, u32[]{:S(2)}, u32[]{:S(2)}) async-start(bf16[8,2,2048]{2,1,0:T(2,128)(2,1)} %reshape.146), calls=%async_computation.2 | async-start | bytes 131072 | tf_op jit(solution)/shard_map/all_to_all | solution.py:53
  34.9 5.8 %all_gather.12 = bf16[8,32,512]{2,1,0:T(8,128)(2,1)S(1)} all-gather(bf16[8,32,128]{2,1,0:T(8,128)(2,1)S(1)} %copy.28), channel_id=1, replica_groups=mesh['row'=8,'col'=4] {'col'}, dimensions={2}, use_global_device_ids=true | all-gather | bytes 327680 | tf_op jit(solution)/shard_map/all_gather | solution.py:56
  40.8 1.2 %fusion.27 = f32[8,32,128]{2,1,0:T(8,128)S(1)} fusion(bf16[8,32,512]{2,1,0:T(8,128)(2,1)S(1)} %all_gather.12, s32[128]{0:T(128)S(1)} %iota_add_fusion.1), kind=kOutput, calls=%fused_computation.47 | convolution fusion | flops 34537472 | bytes 393728 | tf_op jit(solution)/shard_map/crn,nk->crk/dot_general | solution.py:22
  41.9 1.2 %fusion.35 = f32[8,32,128]{2,1,0:T(8,128)S(1)} fusion(bf16[8,32,512]{2,1,0:T(8,128)(2,1)S(1)} %all_gather.12, s32[128]{0:T(128)S(1)} %iota_add_fusion.1), kind=kOutput, calls=%fused_computation.50 | convolution fusion | flops 34537472 | bytes 393728 | tf_op jit(solution)/shard_map/crn,nk->crk/dot_general | solution.py:22
  44.0 5.9 %all_gather.13 = bf16[8,32,512]{2,1,0:T(8,128)(2,1)S(1)} all-gather(bf16[8,32,128]{2,1,0:T(8,128)(2,1)S(1)} %copy.31), channel_id=1, replica_groups=mesh['row'=8,'col'=4] {'col'}, dimensions={2}, use_global_device_ids=true | all-gather | bytes 327680 | tf_op jit(solution)/shard_map/all_gather | solution.py:57
  49.9 1.2 %convolution_add_fusion.1 = f32[8,32,128]{2,1,0:T(8,128)S(1)} fusion(f32[8,32,128]{2,1,0:T(8,128)S(1)} %fusion.27, bf16[8,32,512]{2,1,0:T(8,128)(2,1)S(1)} %all_gather.13, s32[128]{0:T(128)S(1)} %iota_add_fusion.1), kind=kOutput, calls=%fused_computation.2 | convolution fusion | flops 34570240 | bytes 524800 | tf_op jit(solution)/shard_map/crn,nk->crk/dot_general | solution.py:22
  51.1 1.2 %fusion.17 = (bf16[8,32,128]{2,1,0:T(8,128)(2,1)S(1)}, bf16[8,32,128]{2,1,0:T(8,128)(2,1)S(1)}) fusion(bf16[8,32,128]{2,1,0:T(8,128)(2,1)S(1)} %copy-done, f32[8,32,128]{2,1,0:T(8,128)S(1)} %convolution_add_fusion.1, bf16[8,32,128]{2,1,0:T(8,128)(2,1)S(1)} %copy-done.1, f32[8,32,128]{2,1,0:T(8,128)S(1)} %fusion.35, bf16[8,32,512]{2,1,0:T(8,128)(2,1)S(1)} %all_gather.13, ...), kind=kOutput, calls=%fused_computation.36 | convolution fusion | flops 34897920 | bytes 786944 | tf_op jit(solution)/shard_map/crn,nk->crk/dot_general | solution.py:22
  52.3 6.1 %all_gather.14 = bf16[8,32,512]{2,1,0:T(8,128)(2,1)S(1)} all-gather(bf16[8,32,128]{2,1,0:T(8,128)(2,1)S(1)} %get-tuple-element.5), channel_id=1, replica_groups=mesh['row'=8,'col'=4] {'col'}, dimensions={2}, use_global_device_ids=true | all-gather | bytes 327680 | tf_op jit(solution)/shard_map/all_gather | solution.py:69
  58.4 1.2 %fusion.32 = f32[8,32,128]{2,1,0:T(8,128)S(1)} fusion(bf16[8,32,512]{2,1,0:T(8,128)(2,1)S(1)} %all_gather.14, s32[128]{0:T(128)S(1)} %iota_add_fusion.1), kind=kOutput, calls=%fused_computation.49 | convolution fusion | flops 34537472 | bytes 393728 | tf_op jit(solution)/shard_map/crn,nk->crk/dot_general | solution.py:22
  59.5 5.9 %all_gather.15 = bf16[8,32,512]{2,1,0:T(8,128)(2,1)S(1)} all-gather(bf16[8,32,128]{2,1,0:T(8,128)(2,1)S(1)} %get-tuple-element.6), channel_id=1, replica_groups=mesh['row'=8,'col'=4] {'col'}, dimensions={2}, use_global_device_ids=true | all-gather | bytes 327680 | tf_op jit(solution)/shard_map/all_gather | solution.py:70
  65.4 1.2 %fusion.30 = f32[8,32,128]{2,1,0:T(8,128)S(1)} fusion(bf16[8,32,512]{2,1,0:T(8,128)(2,1)S(1)} %all_gather.15, s32[128]{0:T(128)S(1)} %iota_add_fusion.1), kind=kOutput, calls=%fused_computation.48 | convolution fusion | flops 34537472 | bytes 393728 | tf_op jit(solution)/shard_map/crn,nk->crk/dot_general | solution.py:22
  66.6 1.2 %convolution_subtract_fusion = f32[8,32,128]{2,1,0:T(8,128)S(1)} fusion(f32[8,32,128]{2,1,0:T(8,128)S(1)} %fusion.30, bf16[8,32,512]{2,1,0:T(8,128)(2,1)S(1)} %all_gather.14, s32[128]{0:T(128)S(1)} %iota_add_fusion.1), kind=kOutput, calls=%fused_computation | convolution fusion | flops 34570240 | bytes 524800 | tf_op jit(solution)/shard_map/crn,nk->crk/dot_general | solution.py:22
  67.8 1.2 %subtract_convert_fusion = (bf16[8,32,128]{2,1,0:T(8,128)(2,1)S(1)}, bf16[8,32,128]{2,1,0:T(8,128)(2,1)S(1)}) fusion(f32[8,32,128]{2,1,0:T(8,128)S(1)} %convolution_subtract_fusion, f32[32,128]{1,0:T(8,128)S(1)} %get-tuple-element.12, f32[32,128]{1,0:T(8,128)S(1)} %get-tuple-element.11, f32[8,32,128]{2,1,0:T(8,128)S(1)} %fusion.32, ...), kind=kOutput, calls=%fused_computation.44 | convolution fusion | flops 34832384 | bytes 688640 | tf_op jit(solution)/shard_map/crn,nk->crk/dot_general | solution.py:22
  70.1 5.9 %all-to-all-start.4 = ((bf16[8,2,2048]{2,1,0:T(2,128)(2,1)}), bf16[8,2,2048]{2,1,0:T(2,128)(2,1)S(1)}, u32[]{:S(2)}, u32[]{:S(2)}) async-start(bf16[8,2,2048]{2,1,0:T(2,128)(2,1)} %reshape.150), calls=%async_computation.4 | async-start | bytes 131072 | tf_op jit(solution)/shard_map/all_to_all | solution.py:81
  77.1 5.8 %all-to-all-done.4 = bf16[8,2,2048]{2,1,0:T(2,128)(2,1)S(1)} async-done(((bf16[8,2,2048]{2,1,0:T(2,128)(2,1)}), bf16[8,2,2048]{2,1,0:T(2,128)(2,1)S(1)}, u32[]{:S(2)}, u32[]{:S(2)}) %all-to-all-start.4) | async-done | bytes 65568 | tf_op jit(solution)/shard_map/all_to_all | solution.py:81
  82.9 3.4 %all-to-all-start.3 = ((bf16[8,2,2048]{2,1,0:T(2,128)(2,1)}), bf16[8,2,2048]{2,1,0:T(2,128)(2,1)S(1)}, u32[]{:S(2)}, u32[]{:S(2)}) async-start(bf16[8,2,2048]{2,1,0:T(2,128)(2,1)} %reshape.148), calls=%async_computation.3 | async-start | bytes 131072 | tf_op jit(solution)/shard_map/all_to_all | solution.py:80
  86.8 6.3 %all-to-all-done.3 = bf16[8,2,2048]{2,1,0:T(2,128)(2,1)S(1)} async-done(((bf16[8,2,2048]{2,1,0:T(2,128)(2,1)}), bf16[8,2,2048]{2,1,0:T(2,128)(2,1)S(1)}, u32[]{:S(2)}, u32[]{:S(2)}) %all-to-all-start.3) | async-done | bytes 65568 | tf_op jit(solution)/shard_map/all_to_all | solution.py:80
  96.8 9.3 %all_to_all.108 = bf16[8,2,2048]{2,1,0:T(2,128)(2,1)S(1)} all-to-all(bf16[8,2,2048]{2,1,0:T(2,128)(2,1)S(1)} %reshape.152), channel_id=1, replica_groups=mesh['row'=8,'col'=4] {'row'}, dimensions={0} | all-to-all | bytes 131072 | tf_op jit(solution)/shard_map/all_to_all | solution.py:87
  (45 shorter events, 15.3 us)
Async XLA Ops:
  1.9 14.2 %all-to-all-start = ((bf16[8,2,2048]{2,1,0:T(2,128)(2,1)}), bf16[8,2,2048]{2,1,0:T(2,128)(2,1)S(1)}, u32[]{:S(2)}, u32[]{:S(2)}) async-start(bf16[8,2,2048]{2,1,0:T(2,128)(2,1)} %reshape.142), calls=%async_computation | async-start | bytes 131072 | tf_op jit(solution)/shard_map/all_to_all | solution.py:45
  20.5 10.2 %all-to-all-start.1 = ((bf16[8,2,2048]{2,1,0:T(2,128)(2,1)}), bf16[8,2,2048]{2,1,0:T(2,128)(2,1)S(1)}, u32[]{:S(2)}, u32[]{:S(2)}) async-start(bf16[8,2,2048]{2,1,0:T(2,128)(2,1)} %reshape.144), calls=%async_computation.1 | async-start | bytes 131072 | tf_op jit(solution)/shard_map/all_to_all | solution.py:52
  30.7 12.4 %all-to-all-start.2 = ((bf16[8,2,2048]{2,1,0:T(2,128)(2,1)}), bf16[8,2,2048]{2,1,0:T(2,128)(2,1)S(1)}, u32[]{:S(2)}, u32[]{:S(2)}) async-start(bf16[8,2,2048]{2,1,0:T(2,128)(2,1)} %reshape.146), calls=%async_computation.2 | async-start | bytes 131072 | tf_op jit(solution)/shard_map/all_to_all | solution.py:53
  49.9 1.2 %copy-start = (bf16[8,32,128]{2,1,0:T(8,128)(2,1)S(1)}, bf16[8,32,128]{2,1,0:T(8,128)(2,1)}, u32[]{:S(2)}) copy-start(bf16[8,32,128]{2,1,0:T(8,128)(2,1)} %param.5) | copy-start | bytes 196612
  49.9 1.2 %copy-start.1 = (bf16[8,32,128]{2,1,0:T(8,128)(2,1)S(1)}, bf16[8,32,128]{2,1,0:T(8,128)(2,1)}, u32[]{:S(2)}) copy-start(bf16[8,32,128]{2,1,0:T(8,128)(2,1)} %param.6) | copy-start | bytes 196612
  70.1 12.8 %all-to-all-start.4 = ((bf16[8,2,2048]{2,1,0:T(2,128)(2,1)}), bf16[8,2,2048]{2,1,0:T(2,128)(2,1)S(1)}, u32[]{:S(2)}, u32[]{:S(2)}) async-start(bf16[8,2,2048]{2,1,0:T(2,128)(2,1)} %reshape.150), calls=%async_computation.4 | async-start | bytes 131072 | tf_op jit(solution)/shard_map/all_to_all | solution.py:81
  82.9 10.2 %all-to-all-start.3 = ((bf16[8,2,2048]{2,1,0:T(2,128)(2,1)}), bf16[8,2,2048]{2,1,0:T(2,128)(2,1)S(1)}, u32[]{:S(2)}, u32[]{:S(2)}) async-start(bf16[8,2,2048]{2,1,0:T(2,128)(2,1)} %reshape.148), calls=%async_computation.3 | async-start | bytes 131072 | tf_op jit(solution)/shard_map/all_to_all | solution.py:80
  93.6 1.1 %copy-start.2 = (f32[8]{0:T(128)S(1)}, f32[8]{0:T(128)}, u32[]{:S(2)}) copy-start(f32[8]{0:T(128)} %param.7) | copy-start | bytes 100
where the time goes:
time: 108 us
  blocking collectives  33 us (31%)
  waiting for transfers between devices  24 us (22%)
  starting transfers between devices  23.3 us (22%)
  matrix products  13.7 us (13%)
  local copies, waits for them, and re-layouts  12.9 us (12%)
    all_to_all x1, blocking collectives, local(): lax.all_to_all(pair_out, 'row', split_axis=1, concat_axis=2, tiled=True)  9.29 us
    dot_general x8, matrix products, column_product(): jnp.einsum('crn,nk->crk', series, phase, preferred_element_type=jnp.float32)  9.28 us
    unnamed x19, local copies, waits for them, and re-layouts  8.34 us
    all_to_all x1, starting transfers between devices, local(): lax.all_to_all(signal, 'row', split_axis=2, concat_axis=1, tiled=True)  7.31 us
    all_to_all x1, waiting for transfers between devices, local(): lax.all_to_all(signal, 'row', split_axis=2, concat_axis=1, tiled=True)  6.72 us
    all_to_all x1, waiting for transfers between devices, local(): lax.all_to_all(unwound_re, 'row', split_axis=2, concat_axis=1, tiled=True)  6.29 us
    all_gather x1, blocking collectives, local(): lax.all_gather(prod_re, 'col', axis=2, tiled=True)  6.09 us
    all_to_all x1, starting transfers between devices, local(): lax.all_to_all(unwound_im, 'row', split_axis=2, concat_axis=1, tiled=True)  5.93 us
  transfers between devices with their start and end apart: 5, of which 4 were waited for; matrix products, arithmetic and copies ran while one was open for 6% of the time, Pallas kernels for 0%

commit v1 on v0

--- a/solution.py
+++ b/solution.py
@@ -1,8 +1,12 @@
+import functools
 import math
 
 import jax
 import jax.numpy as jnp
+import numpy as np
 from jax import lax
+from jax.experimental import pallas as pl
+from jax.experimental.pallas import tpu as pltpu
 from jax.sharding import PartitionSpec as P
 
 
@@ -26,7 +30,7 @@
     return jnp.einsum("rn,cnj->crj", phase, series, preferred_element_type=jnp.float32)
 
 
-def local(signal, filter_real, filter_imag, skip):
+def local_by_columns(signal, filter_real, filter_imag, skip):
     channels, row_count, col_count = signal.shape
     first_len = row_count * lax.axis_size("row")
     second_len = col_count * lax.axis_size("col")
@@ -52,26 +56,16 @@
         lax.all_to_all(pair_mix_re, "row", split_axis=1, concat_axis=2, tiled=True),
         lax.all_to_all(pair_mix_im, "row", split_axis=1, concat_axis=2, tiled=True),
     )
-    pieces = (
-        lax.all_gather(mixed_re, "col", axis=2, tiled=True),
-        lax.all_gather(mixed_im, "col", axis=2, tiled=True),
-    )
-    amount = pieces[0].shape[2]
-    phase_re, phase_im = phase_table(jnp.arange(amount, dtype=jnp.int32), own_cols, second_len)
-    part_re, part_im = pieces
-    new_re = column_product(part_re, phase_re) - column_product(part_im, phase_im)
-    new_im = column_product(part_re, phase_im) + column_product(part_im, phase_re)
-    spec_re = new_re
-    spec_im = new_im
+    part_re = lax.all_gather(mixed_re, "col", axis=2, tiled=True)
+    part_im = lax.all_gather(mixed_im, "col", axis=2, tiled=True)
+    all_cols = jnp.arange(second_len, dtype=jnp.int32)
+    phase_re, phase_im = phase_table(all_cols, own_cols, second_len)
+    spec_re = column_product(part_re, phase_re) - column_product(part_im, phase_im)
+    spec_im = column_product(part_re, phase_im) + column_product(part_im, phase_re)
     prod_re = (spec_re * filter_real - spec_im * filter_imag).astype(jnp.bfloat16)
     prod_im = (spec_re * filter_imag + spec_im * filter_real).astype(jnp.bfloat16)
-    pieces = (
-        lax.all_gather(prod_re, "col", axis=2, tiled=True),
-        lax.all_gather(prod_im, "col", axis=2, tiled=True),
-    )
-    amount = pieces[0].shape[2]
-    phase_re, phase_im = phase_table(jnp.arange(amount, dtype=jnp.int32), own_cols, second_len)
-    part_re, part_im = pieces
+    part_re = lax.all_gather(prod_re, "col", axis=2, tiled=True)
+    part_im = lax.all_gather(prod_im, "col", axis=2, tiled=True)
     new_re = column_product(part_re, phase_re) + column_product(part_im, phase_im)
     new_im = column_product(part_im, phase_re) - column_product(part_re, phase_im)
     unwound_re = (new_re * twist_re + new_im * twist_im).astype(jnp.bfloat16)
@@ -87,6 +81,141 @@
     return lax.all_to_all(pair_out, "row", split_axis=1, concat_axis=2, tiled=True)
 
 
+def numpy_phase(left_ids, right_ids, modulus):
+    product = (left_ids[:, None].astype(np.int64) * right_ids[None, :]) % modulus
+    angle = np.float32(-2.0 * math.pi / modulus) * product.astype(np.float32)
+    return np.cos(angle), np.sin(angle)
+
+
+def tables(first_len, second_len, row_count, parts):
+    height = row_count // parts
+    rows = np.arange(first_len)
+    cols = np.arange(second_len)
+    first = np.stack(numpy_phase(rows, rows, first_len))
+    twist = np.stack(numpy_phase(rows, cols, first_len * second_len))
+
+    def by_part(table):
+        width = table.shape[-1]
+        cut = table.reshape(2, first_len // row_count, parts, height, width)
+        return cut.transpose(2, 0, 1, 3, 4).reshape(parts, -1, width)
+
+    second = np.concatenate(numpy_phase(cols, cols, second_len), axis=1)
+    return (
+        jnp.asarray(by_part(first), jnp.bfloat16),
+        jnp.asarray(by_part(twist), jnp.float32),
+        jnp.asarray(second, jnp.bfloat16),
+    )
+
+
+def spectrum_kernel(part_ref, got_ref, first_ref, twist_ref, second_ref, out_ref, *, rows, parts, row_count):
+    del part_ref
+    height = row_count // parts
+    mine = rows * height
+    first_len = rows * row_count
+    col_count = got_ref.shape[-1]
+    second_len = parts * col_count
+    seq_len = first_len * second_len
+    first = first_ref[0]
+    twist_re = twist_ref[0, :mine]
+    twist_im = twist_ref[0, mine:]
+
+    def dot(left, right, dims=((1,), (0,))):
+        return lax.dot_general(left, right, (dims, ((), ())), preferred_element_type=jnp.float32)
+
+    series = jnp.concatenate(
+        [got_ref[:, part, :row_count, :].reshape(first_len, col_count) for part in range(parts)], axis=1
+    )
+    half = dot(first, series)
+    half_re, half_im = half[:mine], half[mine:]
+    mixed = jnp.concatenate(
+        [half_re * twist_re - half_im * twist_im, half_re * twist_im + half_im * twist_re], axis=0
+    ).astype(jnp.bfloat16)
+    both = dot(mixed, second_ref[...])
+    spec_re = both[:mine, :second_len] - both[mine:, second_len:]
+    spec_im = both[:mine, second_len:] + both[mine:, :second_len]
+
+    def filter_part(start):
+        return jnp.concatenate(
+            [
+                got_ref[:, part, start : start + height, :].astype(jnp.float32).reshape(mine, col_count)
+                for part in range(parts)
+            ],
+            axis=1,
+        )
+
+    filt_re = filter_part(row_count)
+    filt_im = filter_part(row_count + height)
+    prod = jnp.concatenate(
+        [spec_re * filt_re - spec_im * filt_im, spec_re * filt_im + spec_im * filt_re], axis=0
+    ).astype(jnp.bfloat16)
+    both = dot(prod, second_ref[...])
+    back_re = both[:mine, :second_len] + both[mine:, second_len:]
+    back_im = both[mine:, :second_len] - both[:mine, second_len:]
+    unwound = jnp.concatenate(
+        [back_re * twist_re + back_im * twist_im, back_im * twist_re - back_re * twist_im], axis=0
+    ).astype(jnp.bfloat16)
+    total = dot(first, unwound, ((0,), (0,))) / seq_len
+    total = total.astype(jnp.bfloat16)
+    for part in range(parts):
+        piece = total[:, part * col_count : (part + 1) * col_count]
+        out_ref[:, part] = piece.reshape(rows, row_count, col_count)
+
+
+def local_by_channels(signal, filter_real, filter_imag, skip):
+    channels, row_count, col_count = signal.shape
+    rows = lax.axis_size("row")
+    parts = lax.axis_size("col")
+    share = channels // rows
+    height = row_count // parts
+    first, twist, second = tables(rows * row_count, parts * col_count, row_count, parts)
+    part = lax.axis_index("col").astype(jnp.int32).reshape(1)
+    outs = []
+    for turn in range(share):
+        own = slice(turn * rows, (turn + 1) * rows)
+        send = jnp.concatenate(
+            [
+                jnp.broadcast_to(signal[own][:, None], (rows, parts, row_count, col_count)),
+                filter_real[own].reshape(rows, parts, height, col_count),
+                filter_imag[own].reshape(rows, parts, height, col_count),
+            ],
+            axis=2,
+        )
+        tall = send.shape[2]
+        got = lax.all_to_all(
+            send.reshape(rows * parts, tall, col_count), ("row", "col"), 0, 0, tiled=True
+        ).reshape(rows, parts, tall, col_count)
+        kernel = functools.partial(spectrum_kernel, rows=rows, parts=parts, row_count=row_count)
+        partial_sums = pl.pallas_call(
+            kernel,
+            out_shape=jax.ShapeDtypeStruct((rows, parts, row_count, col_count), jnp.bfloat16),
+            grid_spec=pltpu.PrefetchScalarGridSpec(
+                num_scalar_prefetch=1,
+                grid=(1,),
+                in_specs=[
+                    pl.BlockSpec(got.shape, lambda i, p: (0, 0, 0, 0)),
+                    pl.BlockSpec((1,) + first.shape[1:], lambda i, p: (p[0], 0, 0)),
+                    pl.BlockSpec((1,) + twist.shape[1:], lambda i, p: (p[0], 0, 0)),
+                    pl.BlockSpec(second.shape, lambda i, p: (0, 0)),
+                ],
+                out_specs=pl.BlockSpec((rows, parts, row_count, col_count), lambda i, p: (0, 0, 0, 0)),
+            ),
+        )(part, got, first, twist, second)
+        back = lax.all_to_all(
+            partial_sums.reshape(rows * parts, row_count, col_count), ("row", "col"), 0, 0, tiled=True
+        ).reshape(rows, parts, row_count, col_count)
+        total = jnp.sum(back.astype(jnp.float32), axis=1)
+        outs.append((total + skip[own, None, None] * signal[own].astype(jnp.float32)).astype(jnp.bfloat16))
+    return outs[0] if share == 1 else jnp.concatenate(outs, axis=0)
+
+
+def local(signal, filter_real, filter_imag, skip):
+    channels, row_count, _ = signal.shape
+    whole_shares = channels % lax.axis_size("row") == 0
+    if whole_shares and row_count % (8 * lax.axis_size("col")) == 0:
+        return local_by_channels(signal, filter_real, filter_imag, skip)
+    return local_by_columns(signal, filter_real, filter_imag, skip)
+
+
 def solution(mesh):
     in_specs = (P(None, "row", "col"), P(None, "row", "col"), P(None, "row", "col"), P())
     out_specs = P(None, "row", "col")

time: 108 us -> 41.3 us (0.38)
  blocking collectives: 33 us -> 13.2 us
  starting transfers between devices: 23.3 us -> 7.33 us
  matrix products: 13.7 us -> 0 us
  waiting for transfers between devices: 24 us -> 13.2 us
  local copies, waits for them, and re-layouts: 12.9 us -> 2.47 us
  Pallas kernels: 0 us -> 3.15 us
  other arithmetic: 0.36 us -> 1.53 us
    all_gather x4 -> x0, blocking collectives: 23.7 us -> none  [the longest x1 6.09 us: local(): lax.all_gather(prod_re, 'col', axis=2, tiled=True)]
    all_to_all x5 -> x1, starting transfers between devices: 23.3 us -> 7.33 us  [local_by_channels(): lax.all_to_all(send.reshape(rows * parts, tall, col_count), ('row', 'col'...]
    dot_general x10 -> x0, matrix products: 11.5 us -> none  [the longest x8 9.28 us: column_product(): jnp.einsum('crn,nk->crk', series, phase, preferred_element_type=jnp.float32)]
    all_to_all x5 -> x1, waiting for transfers between devices: 24 us -> 13.2 us  [local_by_channels(): lax.all_to_all(send.reshape(rows * parts, tall, col_count), ('row', 'col'...]
    unnamed x19 -> x10, local copies, waits for them, and re-layouts: 8.34 us -> 1.56 us
    all_to_all x1, blocking collectives: 9.29 us -> 13.2 us  [local_by_channels(): lax.all_to_all(partial_sums.reshape(rows * parts, row_count, col_count),...]
    all_to_all x12 -> x0, local copies, waits for them, and re-layouts: 3.24 us -> none  [the longest x2 1.14 us: local(): lax.all_to_all(pair_out, 'row', split_axis=1, concat_axis=2, tiled=True)]
    pallas_call x0 -> x1, Pallas kernels: none -> 3.15 us  [local_by_channels(): pl.pallas_call(kernel, out_shape=jax.ShapeDtypeStruct((rows, parts, row_c...]
  transfers between devices with their start and end apart: 5 -> 1, of which waited for: 4 -> 1; matrix products, arithmetic and copies ran while one was open for 6% -> 0% of each run, Pallas kernels for 0% -> 0%
where the time goes in v1:
time: 41.3 us; the launch traced here: 40.9 us
  waiting for transfers between devices  13.2 us (32%)
  blocking collectives  13.2 us (32%)
  starting transfers between devices  7.33 us (18%)
  Pallas kernels  3.15 us (8%)
  local copies, waits for them, and re-layouts  2.47 us (6%)
  other arithmetic  1.53 us (4%)
    all_to_all x1, waiting for transfers between devices, local_by_channels(): lax.all_to_all(send.reshape(rows * parts, tall, col_count), ('row', 'col'...  13.2 us
    all_to_all x1, blocking collectives, local_by_channels(): lax.all_to_all(partial_sums.reshape(rows * parts, row_count, col_count),...  13.2 us
    all_to_all x1, starting transfers between devices, local_by_channels(): lax.all_to_all(send.reshape(rows * parts, tall, col_count), ('row', 'col'...  7.33 us
    pallas_call x1, Pallas kernels, local_by_channels(): pl.pallas_call(kernel, out_shape=jax.ShapeDtypeStruct((rows, parts, row_c...  3.15 us
    unnamed x10, local copies, waits for them, and re-layouts  1.56 us
    broadcast_in_dim x1, local copies, waits for them, and re-layouts, local_by_channels(): jnp.broadcast_to(signal[own][:, None], (rows, parts, row_count, col_count))  0.91 us
  transfers between devices with their start and end apart: 1, of which 1 were waited for; matrix products, arithmetic and copies ran while one was open for 0% of the time, Pallas kernels for 0%

profile of v1, /device:TPU:0, one launch (start us, length us, event | category | flops | bytes accessed | tf_op | source)
XLA Modules:
  0.0 40.9 jit_solution(10596453122755917975)
XLA Ops:
  0.0 0.0 copy-start.3
  0.0 0.0 copy-start.2
  0.0 0.9 %broadcast_in_dim.2 = bf16[8,4,32,128]{3,2,1,0:T(8,128)(2,1)S(1)} broadcast(bf16[8,32,128]{2,1,0:T(8,128)(2,1)} %param.7), dimensions={0,2,3} | broadcast | bytes 327680 | tf_op jit(solution)/shard_map/broadcast_in_dim | solution.py:177
  0.9 0.0 copy-done.3
  0.9 0.0 copy-done.2
  0.9 0.8 %pad_maximum_fusion = bf16[32,48,128]{2,1,0:T(8,128)(2,1)} fusion(bf16[32,8,128]{2,1,0:T(8,128)(2,1)S(1)} %bitcast.12, bf16[32,8,128]{2,1,0:T(8,128)(2,1)S(1)} %bitcast.13, bf16[32,32,128]{2,1,0:T(8,128)(2,1)S(1)} %bitcast.10), kind=kLoop, calls=%fused_computation.1 | loop fusion | flops 1179648 | bytes 786432 | tf_op jit(solution)/shard_map/concatenate | solution.py:175
  1.7 7.3 %all-to-all-start = ((bf16[32,48,128]{2,1,0:T(8,128)(2,1)}), bf16[32,48,128]{2,1,0:T(8,128)(2,1)S(1)}, u32[]{:S(2)}, u32[]{:S(2)}) async-start(bf16[32,48,128]{2,1,0:T(8,128)(2,1)} %pad_maximum_fusion), calls=%async_computation | async-start | bytes 786432 | tf_op jit(solution)/shard_map/all_to_all | solution.py:184
  9.1 13.2 %all-to-all-done = bf16[32,48,128]{2,1,0:T(8,128)(2,1)S(1)} async-done(((bf16[32,48,128]{2,1,0:T(8,128)(2,1)}), bf16[32,48,128]{2,1,0:T(8,128)(2,1)S(1)}, u32[]{:S(2)}, u32[]{:S(2)}) %all-to-all-start) | async-done | bytes 393248 | tf_op jit(solution)/shard_map/all_to_all | solution.py:184
  22.3 0.0 copy-start
  22.3 0.7 %copy-done = bf16[32,48,128]{2,1,0:T(8,128)(2,1)} copy-done((bf16[32,48,128]{2,1,0:T(8,128)(2,1)}, bf16[32,48,128]{2,1,0:T(8,128)(2,1)S(1)}, u32[]{:S(2)}) %copy-start) | copy-done | bytes 393240
  23.1 3.1 %shard_map.73 = bf16[8,4,32,128]{3,2,1,0:T(8,128)(2,1)} custom-call(s32[1]{0:T(128)} %bitcast.part_ref, bf16[8,4,48,128]{3,2,1,0:T(8,128)(2,1)} %bitcast.9, bf16[4,128,256]{2,1,0:T(8,128)(2,1)} %constant.12.clone.first_ref, f32[4,128,512]{2,1,0:T(8,128)} %constant.13.clone.twist_ref, bf16[512,1024]{1,0:T(8,128)(2,1)} %constant.14.clone.second_ref), custom_call_target="tpu_custom_call" | custom-call | tf_op jit(solution)/shard_map/pallas_call | solution.py:188
  26.2 13.2 %all_to_all.10 = bf16[32,32,128]{2,1,0:T(8,128)(2,1)S(1)} all-to-all(bf16[32,32,128]{2,1,0:T(8,128)(2,1)} %bitcast.11), channel_id=1, replica_groups=mesh['row'=8,'col'=4] {'row','col'}, dimensions={0} | all-to-all | bytes 524288 | tf_op jit(solution)/shard_map/all_to_all | solution.py:203
  39.4 0.0 copy-start.1
  39.4 0.0 copy-start.4
  39.4 0.8 %copy-done.1 = bf16[8,32,128]{2,1,0:T(8,128)(2,1)S(1)} copy-done((bf16[8,32,128]{2,1,0:T(8,128)(2,1)S(1)}, bf16[8,32,128]{2,1,0:T(8,128)(2,1)}, u32[]{:S(2)}) %copy-start.1) | copy-done | bytes 65560
  40.2 0.0 copy-done.4
  40.2 0.7 %add_convert_fusion = bf16[8,32,128]{2,1,0:T(8,128)(2,1)} fusion(f32[8,32,128]{2,1,0:T(8,128)S(1)} %convert_reduce_fusion, bf16[8,32,128]{2,1,0:T(8,128)(2,1)S(1)} %copy-done.1, f32[8]{0:T(128)S(1)} %copy-done.4), kind=kLoop, calls=%fused_computation.2 | loop fusion | flops 131072 | bytes 262176 | tf_op jit(solution)/shard_map/convert_element_type | solution.py:207
  (1 shorter events, 0.0 us)
Async XLA Ops:
  0.0 0.9 %copy-start.3 = (bf16[8,32,128]{2,1,0:T(8,128)(2,1)S(1)}, bf16[8,32,128]{2,1,0:T(8,128)(2,1)}, u32[]{:S(2)}) copy-start(bf16[8,32,128]{2,1,0:T(8,128)(2,1)} %param.8) | copy-start | bytes 196612
  0.0 0.9 %copy-start.2 = (bf16[8,32,128]{2,1,0:T(8,128)(2,1)S(1)}, bf16[8,32,128]{2,1,0:T(8,128)(2,1)}, u32[]{:S(2)}) copy-start(bf16[8,32,128]{2,1,0:T(8,128)(2,1)} %param.9) | copy-start | bytes 196612
  1.7 20.6 %all-to-all-start = ((bf16[32,48,128]{2,1,0:T(8,128)(2,1)}), bf16[32,48,128]{2,1,0:T(8,128)(2,1)S(1)}, u32[]{:S(2)}, u32[]{:S(2)}) async-start(bf16[32,48,128]{2,1,0:T(8,128)(2,1)} %pad_maximum_fusion), calls=%async_computation | async-start | bytes 786432 | tf_op jit(solution)/shard_map/all_to_all | solution.py:184
  22.3 0.7 %copy-start = (bf16[32,48,128]{2,1,0:T(8,128)(2,1)}, bf16[32,48,128]{2,1,0:T(8,128)(2,1)S(1)}, u32[]{:S(2)}) copy-start(bf16[32,48,128]{2,1,0:T(8,128)(2,1)S(1)} %all-to-all-done) | copy-start | bytes 1179652
  39.4 0.8 %copy-start.1 = (bf16[8,32,128]{2,1,0:T(8,128)(2,1)S(1)}, bf16[8,32,128]{2,1,0:T(8,128)(2,1)}, u32[]{:S(2)}) copy-start(bf16[8,32,128]{2,1,0:T(8,128)(2,1)} %param.7) | copy-start | bytes 196612
  39.4 0.8 %copy-start.4 = (f32[8]{0:T(128)S(1)}, f32[8]{0:T(128)}, u32[]{:S(2)}) copy-start(f32[8]{0:T(128)} %param.10) | copy-start | bytes 100

commit v2 on v1

--- a/solution.py
+++ b/solution.py
@@ -1,4 +1,3 @@
-import functools
 import math
 
 import jax
@@ -89,76 +88,119 @@
 
 def tables(first_len, second_len, row_count, parts):
     height = row_count // parts
+    half = row_count // 2
     rows = np.arange(first_len)
     cols = np.arange(second_len)
-    first = np.stack(numpy_phase(rows, rows, first_len))
-    twist = np.stack(numpy_phase(rows, cols, first_len * second_len))
-
-    def by_part(table):
-        width = table.shape[-1]
-        cut = table.reshape(2, first_len // row_count, parts, height, width)
-        return cut.transpose(2, 0, 1, 3, 4).reshape(parts, -1, width)
-
+    blocks = rows.reshape(-1, row_count)
+    first_re, first_im = numpy_phase(rows, rows, first_len)
+    twist_re, twist_im = numpy_phase(rows, cols, first_len * second_len)
+    first, twist, inverse = [], [], []
+    for part in range(parts):
+        own, other = (blocks[:, p * height : (p + 1) * height].reshape(-1) for p in (part, part ^ 1))
+        near, far = (blocks[:, h * half : (h + 1) * half].reshape(-1) for h in (part % 2, 1 - part % 2))
+        order = np.concatenate([near, far])
+        first.append(np.concatenate([first_re[np.ix_(own, order)], first_im[np.ix_(own, order)]]))
+        twist.append(np.concatenate([twist_re[own], twist_im[own]]))
+        inverse.append(
+            np.concatenate([t[np.ix_(near, ids)] for ids in (own, other) for t in (first_re, first_im)], axis=1)
+        )
     second = np.concatenate(numpy_phase(cols, cols, second_len), axis=1)
     return (
-        jnp.asarray(by_part(first), jnp.bfloat16),
-        jnp.asarray(by_part(twist), jnp.float32),
+        jnp.asarray(np.stack(first), jnp.bfloat16),
+        jnp.asarray(np.stack(twist), jnp.float32),
+        jnp.asarray(np.stack(inverse), jnp.bfloat16),
         jnp.asarray(second, jnp.bfloat16),
     )
 
 
-def spectrum_kernel(part_ref, got_ref, first_ref, twist_ref, second_ref, out_ref, *, rows, parts, row_count):
-    del part_ref
+def dot(left, right):
+    return jnp.dot(left, right, preferred_element_type=jnp.float32)
+
+
+def pack_kernel(signal_ref, real_ref, imag_ref, send_ref, sems):
+    rows, parts, _, _ = send_ref.shape
+    row_count, col_count = signal_ref.shape[-2:]
+    half = row_count // 2
     height = row_count // parts
-    mine = rows * height
-    first_len = rows * row_count
-    col_count = got_ref.shape[-1]
+    copies = []
+    for part in range(parts):
+        start = part % 2 * half
+        copies.append((signal_ref.at[:, start : start + half], send_ref.at[:, part, :half]))
+        cut = slice(part * height, (part + 1) * height)
+        copies.append((real_ref.at[:, cut], send_ref.at[:, part, half : half + height]))
+        copies.append((imag_ref.at[:, cut], send_ref.at[:, part, half + height :]))
+    copies = [pltpu.make_async_copy(a, b, sems.at[i]) for i, (a, b) in enumerate(copies)]
+    for copy in copies:
+        copy.start()
+    for copy in copies:
+        copy.wait()
+
+
+def spectrum_kernel(got_ref, swapped_ref, first_ref, twist_ref, second_ref, out_ref):
+    rows, parts, _, col_count = got_ref.shape
     second_len = parts * col_count
-    seq_len = first_len * second_len
-    first = first_ref[0]
-    twist_re = twist_ref[0, :mine]
-    twist_im = twist_ref[0, mine:]
-
-    def dot(left, right, dims=((1,), (0,))):
-        return lax.dot_general(left, right, (dims, ((), ())), preferred_element_type=jnp.float32)
-
-    series = jnp.concatenate(
-        [got_ref[:, part, :row_count, :].reshape(first_len, col_count) for part in range(parts)], axis=1
-    )
-    half = dot(first, series)
-    half_re, half_im = half[:mine], half[mine:]
-    mixed = jnp.concatenate(
-        [half_re * twist_re - half_im * twist_im, half_re * twist_im + half_im * twist_re], axis=0
-    ).astype(jnp.bfloat16)
-    both = dot(mixed, second_ref[...])
-    spec_re = both[:mine, :second_len] - both[mine:, second_len:]
-    spec_im = both[:mine, second_len:] + both[mine:, :second_len]
-
-    def filter_part(start):
+    half = first_ref.shape[1] // 2 // rows
+    mine = first_ref.shape[0] // 2
+    height = mine // rows
+    twist_re = twist_ref[:mine]
+    twist_im = twist_ref[mine:]
+
+    def columns(ref, start, count, kind):
         return jnp.concatenate(
             [
-                got_ref[:, part, start : start + height, :].astype(jnp.float32).reshape(mine, col_count)
+                ref[:, part, start : start + count, :].astype(kind).reshape(rows * count, col_count)
                 for part in range(parts)
             ],
             axis=1,
         )
 
-    filt_re = filter_part(row_count)
-    filt_im = filter_part(row_count + height)
+    series = jnp.concatenate(
+        [columns(got_ref, 0, half, jnp.bfloat16), columns(swapped_ref, 0, half, jnp.bfloat16)], axis=0
+    )
+    both = dot(first_ref[...], series)
+    half_re, half_im = both[:mine], both[mine:]
+    mixed = jnp.concatenate(
+        [half_re * twist_re - half_im * twist_im, half_re * twist_im + half_im * twist_re], axis=0
+    ).astype(jnp.bfloat16)
+    both = dot(mixed, second_ref[...])
+    spec_re = both[:mine, :second_len] - both[mine:, second_len:]
+    spec_im = both[:mine, second_len:] + both[mine:, :second_len]
+    filt_re = columns(got_ref, half, height, jnp.float32)
+    filt_im = columns(got_ref, half + height, height, jnp.float32)
     prod = jnp.concatenate(
         [spec_re * filt_re - spec_im * filt_im, spec_re * filt_im + spec_im * filt_re], axis=0
     ).astype(jnp.bfloat16)
     both = dot(prod, second_ref[...])
     back_re = both[:mine, :second_len] + both[mine:, second_len:]
     back_im = both[mine:, :second_len] - both[:mine, second_len:]
-    unwound = jnp.concatenate(
+    out_ref[...] = jnp.concatenate(
         [back_re * twist_re + back_im * twist_im, back_im * twist_re - back_re * twist_im], axis=0
     ).astype(jnp.bfloat16)
-    total = dot(first, unwound, ((0,), (0,))) / seq_len
-    total = total.astype(jnp.bfloat16)
+
+
+def inverse_kernel(skips_ref, own_ref, other_ref, inverse_ref, got_ref, out_ref):
+    rows, parts, half, col_count = out_ref.shape
+    seq_len = rows * half * 2 * parts * col_count
+    both = jnp.concatenate([own_ref[...], other_ref[...]], axis=0)
+    total = dot(inverse_ref[...], both) / seq_len
     for part in range(parts):
-        piece = total[:, part * col_count : (part + 1) * col_count]
-        out_ref[:, part] = piece.reshape(rows, row_count, col_count)
+        piece = total[:, part * col_count : (part + 1) * col_count].reshape(rows, half, col_count)
+        series = got_ref[:, part, :half, :].astype(jnp.float32)
+        out_ref[:, part] = (piece + skips_ref[part] * series).astype(jnp.bfloat16)
+
+
+def in_vmem(array):
+    return pltpu.with_memory_space_constraint(array, pltpu.VMEM)
+
+
+def call(kernel, out_shape, *args, **options):
+    return pl.pallas_call(
+        kernel,
+        out_shape=pltpu.VMEM(out_shape, jnp.bfloat16),
+        in_specs=[pl.BlockSpec(memory_space=pltpu.VMEM)] * len(args),
+        out_specs=pl.BlockSpec(memory_space=pltpu.VMEM),
+        **options,
+    )(*map(in_vmem, args))
 
 
 def local_by_channels(signal, filter_real, filter_imag, skip):
@@ -166,52 +208,47 @@
     rows = lax.axis_size("row")
     parts = lax.axis_size("col")
     share = channels // rows
-    height = row_count // parts
-    first, twist, second = tables(rows * row_count, parts * col_count, row_count, parts)
-    part = lax.axis_index("col").astype(jnp.int32).reshape(1)
+    half = row_count // 2
+    tall = half + 2 * (row_count // parts)
+    every = ("row", "col")
+    pairs = [(part, part ^ 1) for part in range(parts)]
+    part = lax.axis_index("col")
+    first, twist, inverse, second = tables(rows * row_count, parts * col_count, row_count, parts)
+    first, twist, inverse = (lax.dynamic_index_in_dim(t, part, 0, keepdims=False) for t in (first, twist, inverse))
     outs = []
     for turn in range(share):
         own = slice(turn * rows, (turn + 1) * rows)
-        send = jnp.concatenate(
-            [
-                jnp.broadcast_to(signal[own][:, None], (rows, parts, row_count, col_count)),
-                filter_real[own].reshape(rows, parts, height, col_count),
-                filter_imag[own].reshape(rows, parts, height, col_count),
-            ],
-            axis=2,
+        send = pl.pallas_call(
+            pack_kernel,
+            out_shape=pltpu.VMEM((rows, parts, tall, col_count), jnp.bfloat16),
+            in_specs=[pl.BlockSpec(memory_space=pl.ANY)] * 3,
+            out_specs=pl.BlockSpec(memory_space=pltpu.VMEM),
+            scratch_shapes=[pltpu.SemaphoreType.DMA((3 * parts,))],
+        )(signal[own], filter_real[own], filter_imag[own])
+        got = lax.all_to_all(send.reshape(rows * parts, tall, col_count), every, 0, 0, tiled=True)
+        got = got.reshape(rows, parts, tall, col_count)
+        swapped = lax.ppermute(got, "col", pairs)
+        unwound = call(
+            spectrum_kernel, first.shape[:1] + (parts * col_count,), got, swapped, first, twist, second
         )
-        tall = send.shape[2]
-        got = lax.all_to_all(
-            send.reshape(rows * parts, tall, col_count), ("row", "col"), 0, 0, tiled=True
-        ).reshape(rows, parts, tall, col_count)
-        kernel = functools.partial(spectrum_kernel, rows=rows, parts=parts, row_count=row_count)
+        other = lax.ppermute(unwound, "col", pairs)
+        skips = jnp.where(jnp.arange(parts) // 2 == part // 2, skip[turn * rows + lax.axis_index("row")], 0.0)
         partial_sums = pl.pallas_call(
-            kernel,
-            out_shape=jax.ShapeDtypeStruct((rows, parts, row_count, col_count), jnp.bfloat16),
-            grid_spec=pltpu.PrefetchScalarGridSpec(
-                num_scalar_prefetch=1,
-                grid=(1,),
-                in_specs=[
-                    pl.BlockSpec(got.shape, lambda i, p: (0, 0, 0, 0)),
-                    pl.BlockSpec((1,) + first.shape[1:], lambda i, p: (p[0], 0, 0)),
-                    pl.BlockSpec((1,) + twist.shape[1:], lambda i, p: (p[0], 0, 0)),
-                    pl.BlockSpec(second.shape, lambda i, p: (0, 0)),
-                ],
-                out_specs=pl.BlockSpec((rows, parts, row_count, col_count), lambda i, p: (0, 0, 0, 0)),
-            ),
-        )(part, got, first, twist, second)
-        back = lax.all_to_all(
-            partial_sums.reshape(rows * parts, row_count, col_count), ("row", "col"), 0, 0, tiled=True
-        ).reshape(rows, parts, row_count, col_count)
-        total = jnp.sum(back.astype(jnp.float32), axis=1)
-        outs.append((total + skip[own, None, None] * signal[own].astype(jnp.float32)).astype(jnp.bfloat16))
+            inverse_kernel,
+            out_shape=pltpu.VMEM((rows, parts, half, col_count), jnp.bfloat16),
+            in_specs=[pl.BlockSpec(memory_space=pltpu.SMEM)] + [pl.BlockSpec(memory_space=pltpu.VMEM)] * 4,
+            out_specs=pl.BlockSpec(memory_space=pltpu.VMEM),
+        )(skips, *map(in_vmem, (unwound, other, inverse, got)))
+        back = lax.all_to_all(partial_sums.reshape(rows * parts, half, col_count), every, 0, 0, tiled=True)
+        back = back.reshape(rows, parts // 2, row_count, col_count)
+        outs.append(jnp.sum(back.astype(jnp.float32), axis=1).astype(jnp.bfloat16))
     return outs[0] if share == 1 else jnp.concatenate(outs, axis=0)
 
 
 def local(signal, filter_real, filter_imag, skip):
     channels, row_count, _ = signal.shape
-    whole_shares = channels % lax.axis_size("row") == 0
-    if whole_shares and row_count % (8 * lax.axis_size("col")) == 0:
+    parts = lax.axis_size("col")
+    if channels % lax.axis_size("row") == 0 and parts % 2 == 0 and row_count % (8 * parts) == 0:
         return local_by_channels(signal, filter_real, filter_imag, skip)
     return local_by_columns(signal, filter_real, filter_imag, skip)
 

time: 41.3 us -> 37.4 us (0.906)
  blocking collectives: 13.2 us -> 28.1 us
  waiting for transfers between devices: 13.2 us -> 0.01 us
  starting transfers between devices: 7.33 us -> 0.57 us
  local copies, waits for them, and re-layouts: 2.47 us -> 3.9 us
  Pallas kernels: 3.15 us -> 2.67 us
    all_to_all x1 -> x2, blocking collectives: 13.2 us -> 28.1 us  [the longest x1 17.7 us: local_by_channels(): lax.all_to_all(send.reshape(rows * parts, tall, col_count), every, 0, 0,...]
    all_to_all x1 -> x0, waiting for transfers between devices: 13.2 us -> none  [local_by_channels(): lax.all_to_all(send.reshape(rows * parts, tall, col_count), ('row', 'col'...]
    all_to_all x1 -> x0, starting transfers between devices: 7.33 us -> none  [local_by_channels(): lax.all_to_all(send.reshape(rows * parts, tall, col_count), ('row', 'col'...]
    squeeze x0 -> x3, local copies, waits for them, and re-layouts: none -> 2.65 us  [local_by_channels(): lax.dynamic_index_in_dim(t, part, 0, keepdims=False)]
    unnamed x10 -> x2, local copies, waits for them, and re-layouts: 1.56 us -> 0.01 us
    dynamic_slice x0 -> x1, local copies, waits for them, and re-layouts: none -> 1.24 us  [local_by_channels(): skip[turn * rows + lax.axis_index('row')]]
    select_n x0 -> x1, other arithmetic: none -> 1.15 us  [local_by_channels(): jnp.where(jnp.arange(parts) // 2 == part // 2, skip[turn * rows + lax.axi...]
    broadcast_in_dim x1 -> x0, local copies, waits for them, and re-layouts: 0.91 us -> none  [local_by_channels(): jnp.broadcast_to(signal[own][:, None], (rows, parts, row_count, col_count))]
  transfers between devices with their start and end apart: 1 -> 2, of which waited for: 1 -> 0; matrix products, arithmetic and copies ran while one was open for 0% -> 14% of each run, Pallas kernels for 0% -> 0%
where the time goes in v2:
time: 37.4 us; the launch traced here: 37.1 us
  blocking collectives  28.1 us (75%)
  local copies, waits for them, and re-layouts  3.9 us (10%)
  Pallas kernels  2.67 us (7%)
  other arithmetic  1.8 us (5%)
  starting transfers between devices  0.57 us (2%)
    all_to_all x1, blocking collectives, local_by_channels(): lax.all_to_all(send.reshape(rows * parts, tall, col_count), every, 0, 0,...  17.7 us
    all_to_all x1, blocking collectives, local_by_channels(): lax.all_to_all(partial_sums.reshape(rows * parts, half, col_count), every...  10.4 us
    squeeze x3, local copies, waits for them, and re-layouts, local_by_channels(): lax.dynamic_index_in_dim(t, part, 0, keepdims=False)  2.65 us
    dynamic_slice x1, local copies, waits for them, and re-layouts, local_by_channels(): skip[turn * rows + lax.axis_index('row')]  1.24 us
    select_n x1, other arithmetic, local_by_channels(): jnp.where(jnp.arange(parts) // 2 == part // 2, skip[turn * rows + lax.axi...  1.15 us
    pallas_call x1, Pallas kernels, local_by_channels(): pl.pallas_call(pack_kernel, out_shape=pltpu.VMEM((rows, parts, tall, col_...  1.08 us
    pallas_call x1, Pallas kernels, local_by_channels(): pl.pallas_call(inverse_kernel, out_shape=pltpu.VMEM((rows, parts, half, c...  0.85 us
  transfers between devices with their start and end apart: 2, of which 0 were waited for; matrix products, arithmetic and copies ran while one was open for 14% of the time, Pallas kernels for 0%

profile of v2, /device:TPU:0, one launch (start us, length us, event | category | flops | bytes accessed | tf_op | source)
XLA Modules:
  0.0 37.1 jit_solution(12223578572594808351)
XLA Ops:
  0.0 0.0 copy-start
  0.0 1.1 %shard_map.82 = bf16[8,4,32,128]{3,2,1,0:T(8,128)(2,1)S(1)} custom-call(bf16[8,32,128]{2,1,0:T(8,128)(2,1)} %signal_ref.1, bf16[8,32,128]{2,1,0:T(8,128)(2,1)} %real_ref.1, bf16[8,32,128]{2,1,0:T(8,128)(2,1)} %imag_ref.1), custom_call_target="tpu_custom_call" | custom-call | tf_op jit(solution)/shard_map/pallas_call | solution.py:221
  1.1 17.7 %all_to_all.10 = bf16[32,32,128]{2,1,0:T(8,128)(2,1)S(1)} all-to-all(bf16[32,32,128]{2,1,0:T(8,128)(2,1)S(1)} %bitcast.14), channel_id=1, replica_groups=mesh['row'=8,'col'=4] {'row','col'}, dimensions={0} | all-to-all | bytes 524288 | tf_op jit(solution)/shard_map/all_to_all | solution.py:228
  18.8 0.0 collective-permute-start
  18.8 1.2 %dynamic_slice.14 = f32[1]{0:T(128)} dynamic-slice(f32[8]{0:T(128)} %param.11, s32[]{:T(128)S(6)} %select_n.26), dynamic_slice_sizes={1} | dynamic-slice | bytes 12 | tf_op jit(solution)/shard_map/dynamic_slice | solution.py:235
  20.0 0.8 %dynamic-slice_bitcast_fusion.2.first_ref = bf16[128,256]{1,0:T(8,128)(2,1)S(1)} fusion(bf16[4,128,256]{2,1,0:T(8,128)(2,1)} %constant.60.clone, s32[]{:T(128)S(6)} %select_n.28), kind=kLoop, calls=%fused_computation.2 | loop fusion | bytes 131076 | tf_op jit(solution)/shard_map/jit(dynamic_index_in_dim)/squeeze | solution.py:217
  20.9 1.0 %dynamic-slice_bitcast_fusion.twist_ref = f32[128,512]{1,0:T(8,128)S(1)} fusion(f32[4,128,512]{2,1,0:T(8,128)} %constant.61.clone, s32[]{:T(128)S(6)} %select_n.28), kind=kLoop, calls=%fused_computation | loop fusion | bytes 524292 | tf_op jit(solution)/shard_map/jit(dynamic_index_in_dim)/squeeze | solution.py:217
  21.9 0.0 collective-permute-done.swapped_ref
  21.9 0.0 copy-done
  21.9 0.7 %shard_map.83.own_ref = bf16[128,512]{1,0:T(8,128)(2,1)S(1)} custom-call(bf16[8,4,32,128]{3,2,1,0:T(8,128)(2,1)S(1)} %bitcast.12, bf16[8,4,32,128]{3,2,1,0:T(8,128)(2,1)S(1)} %collective-permute-done.swapped_ref, bf16[128,256]{1,0:T(8,128)(2,1)S(1)} %dynamic-slice_bitcast_fusion.2.first_ref, f32[128,512]{1,0:T(8,128)S(1)} %dynamic-slice_bitcast_fusion.twist_ref, ...), custom_call_target="tpu_custom_call" | custom-call | tf_op jit(solution)/shard_map/pallas_call | solution.py:197
  22.6 0.6 %collective-permute-start.1 = (bf16[128,512]{1,0:T(8,128)(2,1)S(1)}, bf16[128,512]{1,0:T(8,128)(2,1)S(1)}, u32[]{:S(2)}, u32[]{:S(2)}) collective-permute-start(bf16[128,512]{1,0:T(8,128)(2,1)S(1)} %shard_map.83.own_ref), channel_id=1, source_target_pairs={{0,1},{1,0},{2,3},{3,2},{4,5},{5,4},{6,7},{7,6},{8,9},{9,8},{10,11... | collective-permute-start | bytes 393224 | tf_op jit(solution)/shard_map/ppermute | solution.py:234
  23.2 1.2 %compare_select_fusion.skips_ref = f32[4]{0:T(128)} fusion(f32[]{:T(128)} %bitcast, s32[]{:T(128)S(6)} %select_n.25), kind=kLoop, calls=%fused_computation.3 | loop fusion | flops 40 | bytes 24 | tf_op jit(solution)/shard_map/jit(_where)/select_n | solution.py:235
  24.3 0.8 %dynamic-slice_bitcast_fusion.1.inverse_ref = bf16[128,256]{1,0:T(8,128)(2,1)S(1)} fusion(bf16[4,128,256]{2,1,0:T(8,128)(2,1)} %constant.62.clone, s32[]{:T(128)S(6)} %select_n.28), kind=kLoop, calls=%fused_computation.1 | loop fusion | bytes 131076 | tf_op jit(solution)/shard_map/jit(dynamic_index_in_dim)/squeeze | solution.py:217
  25.2 0.0 collective-permute-done.1.other_ref
  25.2 0.9 %shard_map.84 = bf16[8,4,16,128]{3,2,1,0:T(8,128)(2,1)S(1)} custom-call(f32[4]{0:T(128)} %compare_select_fusion.skips_ref, bf16[128,512]{1,0:T(8,128)(2,1)S(1)} %shard_map.83.own_ref, bf16[128,512]{1,0:T(8,128)(2,1)S(1)} %collective-permute-done.1.other_ref, bf16[128,256]{1,0:T(8,128)(2,1)S(1)} %dynamic-slice_bitcast_fusion.1.inverse_ref, ...), custom_call_target="tpu_custom_call" | custom-call | tf_op jit(solution)/shard_map/pallas_call | solution.py:236
  26.0 10.4 %all_to_all.11 = bf16[32,16,128]{2,1,0:T(8,128)(2,1)S(1)} all-to-all(bf16[32,16,128]{2,1,0:T(8,128)(2,1)S(1)} %bitcast.15), channel_id=1, replica_groups=mesh['row'=8,'col'=4] {'row','col'}, dimensions={0} | all-to-all | bytes 262144 | tf_op jit(solution)/shard_map/all_to_all | solution.py:242
  36.5 0.7 %reduce_sum.12 = bf16[8,32,128]{2,1,0:T(8,128)(2,1)} reduce(bf16[8,2,32,128]{3,2,1,0:T(8,128)(2,1)S(1)} %bitcast.16, bf16[]{:T(256)} %constant.59.clone.1), dimensions={1}, to_apply=%region_0.1 | reduce | flops 32768 | bytes 196610 | tf_op jit(solution)/shard_map/reduce_sum | solution.py:244
Async XLA Ops:
  0.0 21.9 %copy-start = (bf16[512,1024]{1,0:T(8,128)(2,1)S(1)}, bf16[512,1024]{1,0:T(8,128)(2,1)}, u32[]{:S(2)}) copy-start(bf16[512,1024]{1,0:T(8,128)(2,1)} %constant.63.clone.second_ref) | copy-start | bytes 3145732
  18.8 3.1 %collective-permute-start = (bf16[8,4,32,128]{3,2,1,0:T(8,128)(2,1)S(1)}, bf16[8,4,32,128]{3,2,1,0:T(8,128)(2,1)S(1)}, u32[]{:S(2)}, u32[]{:S(2)}) collective-permute-start(bf16[8,4,32,128]{3,2,1,0:T(8,128)(2,1)S(1)} %bitcast.11), channel_id=1, source_target_pairs={{0,1},{1,0},{2,3},{3,2},{4,5},{5,4},{6,7},{7,6},{8,9},{9,8},{10,11... | collective-permute-start | bytes 786440 | tf_op jit(solution)/shard_map/ppermute | solution.py:230
  22.6 2.6 %collective-permute-start.1 = (bf16[128,512]{1,0:T(8,128)(2,1)S(1)}, bf16[128,512]{1,0:T(8,128)(2,1)S(1)}, u32[]{:S(2)}, u32[]{:S(2)}) collective-permute-start(bf16[128,512]{1,0:T(8,128)(2,1)S(1)} %shard_map.83.own_ref), channel_id=1, source_target_pairs={{0,1},{1,0},{2,3},{3,2},{4,5},{5,4},{6,7},{7,6},{8,9},{9,8},{10,11... | collective-permute-start | bytes 393224 | tf_op jit(solution)/shard_map/ppermute | solution.py:234

commit v3 on v2

--- a/solution.py
+++ b/solution.py
@@ -1,3 +1,4 @@
+import functools
 import math
 
 import jax
@@ -93,21 +94,23 @@
     cols = np.arange(second_len)
     blocks = rows.reshape(-1, row_count)
     first_re, first_im = numpy_phase(rows, rows, first_len)
-    twist_re, twist_im = numpy_phase(rows, cols, first_len * second_len)
-    first, twist, inverse = [], [], []
+    first, inverse = [], []
     for part in range(parts):
         own, other = (blocks[:, p * height : (p + 1) * height].reshape(-1) for p in (part, part ^ 1))
         near, far = (blocks[:, h * half : (h + 1) * half].reshape(-1) for h in (part % 2, 1 - part % 2))
         order = np.concatenate([near, far])
         first.append(np.concatenate([first_re[np.ix_(own, order)], first_im[np.ix_(own, order)]]))
-        twist.append(np.concatenate([twist_re[own], twist_im[own]]))
         inverse.append(
             np.concatenate([t[np.ix_(near, ids)] for ids in (own, other) for t in (first_re, first_im)], axis=1)
         )
+    block_twist = np.stack(numpy_phase(blocks[:, 0], cols, first_len * second_len))
+    row_twist = np.stack(numpy_phase(blocks[0], cols, first_len * second_len))
+    row_twist = row_twist.reshape(2, parts, height, second_len).swapaxes(0, 1)
     second = np.concatenate(numpy_phase(cols, cols, second_len), axis=1)
     return (
         jnp.asarray(np.stack(first), jnp.bfloat16),
-        jnp.asarray(np.stack(twist), jnp.float32),
+        jnp.asarray(block_twist, jnp.float32),
+        jnp.asarray(row_twist, jnp.float32),
         jnp.asarray(np.stack(inverse), jnp.bfloat16),
         jnp.asarray(second, jnp.bfloat16),
     )
@@ -136,28 +139,34 @@
         copy.wait()
 
 
-def spectrum_kernel(got_ref, swapped_ref, first_ref, twist_ref, second_ref, out_ref):
+def columns(ref, start, count, kind):
+    rows, parts, _, col_count = ref.shape
+    return jnp.concatenate(
+        [ref[:, part, start : start + count, :].astype(kind).reshape(rows * count, col_count) for part in range(parts)],
+        axis=1,
+    )
+
+
+def near_kernel(got_ref, first_ref, out_ref):
+    count = first_ref.shape[2] // 2
+    series = columns(got_ref, 0, count // got_ref.shape[0], jnp.bfloat16)
+    out_ref[...] = dot(first_ref[lax.axis_index("col"), :, :count], series)
+
+
+def spectrum_kernel(near_ref, got_ref, swapped_ref, first_ref, block_ref, row_ref, second_ref, out_ref):
     rows, parts, _, col_count = got_ref.shape
     second_len = parts * col_count
-    half = first_ref.shape[1] // 2 // rows
-    mine = first_ref.shape[0] // 2
+    count = first_ref.shape[2] // 2
+    half = count // rows
+    mine = first_ref.shape[1] // 2
     height = mine // rows
-    twist_re = twist_ref[:mine]
-    twist_im = twist_ref[mine:]
-
-    def columns(ref, start, count, kind):
-        return jnp.concatenate(
-            [
-                ref[:, part, start : start + count, :].astype(kind).reshape(rows * count, col_count)
-                for part in range(parts)
-            ],
-            axis=1,
-        )
-
-    series = jnp.concatenate(
-        [columns(got_ref, 0, half, jnp.bfloat16), columns(swapped_ref, 0, half, jnp.bfloat16)], axis=0
-    )
-    both = dot(first_ref[...], series)
+    part = lax.axis_index("col")
+    block_re, block_im = block_ref[0][:, None, :], block_ref[1][:, None, :]
+    row_re, row_im = row_ref[part, 0][None], row_ref[part, 1][None]
+    twist_re = (block_re * row_re - block_im * row_im).reshape(mine, second_len)
+    twist_im = (block_re * row_im + block_im * row_re).reshape(mine, second_len)
+
+    both = near_ref[...] + dot(first_ref[part, :, count:], columns(swapped_ref, 0, half, jnp.bfloat16))
     half_re, half_im = both[:mine], both[mine:]
     mixed = jnp.concatenate(
         [half_re * twist_re - half_im * twist_im, half_re * twist_im + half_im * twist_re], axis=0
@@ -178,29 +187,30 @@
     ).astype(jnp.bfloat16)
 
 
-def inverse_kernel(skips_ref, own_ref, other_ref, inverse_ref, got_ref, out_ref):
+def inverse_kernel(own_ref, other_ref, inverse_ref, got_ref, skip_ref, out_ref, *, turn):
     rows, parts, half, col_count = out_ref.shape
     seq_len = rows * half * 2 * parts * col_count
+    mine = lax.axis_index("col")
+    channel = turn * rows + lax.axis_index("row")
+    at = lax.broadcasted_iota(jnp.int32, skip_ref.shape, 1)
+    skip = jnp.sum(jnp.where(at == channel, skip_ref[...], 0.0), axis=1, keepdims=True)
     both = jnp.concatenate([own_ref[...], other_ref[...]], axis=0)
-    total = dot(inverse_ref[...], both) / seq_len
+    total = dot(inverse_ref[mine], both) / seq_len
     for part in range(parts):
-        piece = total[:, part * col_count : (part + 1) * col_count].reshape(rows, half, col_count)
-        series = got_ref[:, part, :half, :].astype(jnp.float32)
-        out_ref[:, part] = (piece + skips_ref[part] * series).astype(jnp.bfloat16)
-
-
-def in_vmem(array):
-    return pltpu.with_memory_space_constraint(array, pltpu.VMEM)
-
-
-def call(kernel, out_shape, *args, **options):
+        piece = total[:, part * col_count : (part + 1) * col_count]
+        series = got_ref[:, part, :half, :].astype(jnp.float32).reshape(rows * half, col_count)
+        term = jnp.where(mine // 2 == part // 2, skip, 0.0) * series
+        out_ref[:, part] = (piece + term).astype(jnp.bfloat16).reshape(rows, half, col_count)
+
+
+def call(kernel, out_shape, *args, kind=jnp.bfloat16, flops=None):
     return pl.pallas_call(
         kernel,
-        out_shape=pltpu.VMEM(out_shape, jnp.bfloat16),
+        out_shape=pltpu.VMEM(out_shape, kind),
         in_specs=[pl.BlockSpec(memory_space=pltpu.VMEM)] * len(args),
         out_specs=pl.BlockSpec(memory_space=pltpu.VMEM),
-        **options,
-    )(*map(in_vmem, args))
+        cost_estimate=flops and pl.CostEstimate(flops=flops, bytes_accessed=0, transcendentals=0),
+    )(*(pltpu.with_memory_space_constraint(arg, pltpu.VMEM) for arg in args))
 
 
 def local_by_channels(signal, filter_real, filter_imag, skip):
@@ -212,9 +222,7 @@
     tall = half + 2 * (row_count // parts)
     every = ("row", "col")
     pairs = [(part, part ^ 1) for part in range(parts)]
-    part = lax.axis_index("col")
-    first, twist, inverse, second = tables(rows * row_count, parts * col_count, row_count, parts)
-    first, twist, inverse = (lax.dynamic_index_in_dim(t, part, 0, keepdims=False) for t in (first, twist, inverse))
+    first, block, row, inverse, second = tables(rows * row_count, parts * col_count, row_count, parts)
     outs = []
     for turn in range(share):
         own = slice(turn * rows, (turn + 1) * rows)
@@ -228,17 +236,19 @@
         got = lax.all_to_all(send.reshape(rows * parts, tall, col_count), every, 0, 0, tiled=True)
         got = got.reshape(rows, parts, tall, col_count)
         swapped = lax.ppermute(got, "col", pairs)
-        unwound = call(
-            spectrum_kernel, first.shape[:1] + (parts * col_count,), got, swapped, first, twist, second
+        shape = (first.shape[1], parts * col_count)
+        near = call(near_kernel, shape, got, first, kind=jnp.float32, flops=10**9)
+        unwound = call(spectrum_kernel, shape, near, got, swapped, first, block, row, second)
+        other = lax.ppermute(unwound, "col", pairs)
+        partial_sums = call(
+            functools.partial(inverse_kernel, turn=turn),
+            (rows, parts, half, col_count),
+            unwound,
+            other,
+            inverse,
+            got,
+            skip[None],
         )
-        other = lax.ppermute(unwound, "col", pairs)
-        skips = jnp.where(jnp.arange(parts) // 2 == part // 2, skip[turn * rows + lax.axis_index("row")], 0.0)
-        partial_sums = pl.pallas_call(
-            inverse_kernel,
-            out_shape=pltpu.VMEM((rows, parts, half, col_count), jnp.bfloat16),
-            in_specs=[pl.BlockSpec(memory_space=pltpu.SMEM)] + [pl.BlockSpec(memory_space=pltpu.VMEM)] * 4,
-            out_specs=pl.BlockSpec(memory_space=pltpu.VMEM),
-        )(skips, *map(in_vmem, (unwound, other, inverse, got)))
         back = lax.all_to_all(partial_sums.reshape(rows * parts, half, col_count), every, 0, 0, tiled=True)
         back = back.reshape(rows, parts // 2, row_count, col_count)
         outs.append(jnp.sum(back.astype(jnp.float32), axis=1).astype(jnp.bfloat16))

time: 37.4 us -> 34 us (0.909)
  local copies, waits for them, and re-layouts: 3.9 us -> 0.03 us
  waiting for transfers between devices: 0.01 us -> 2.55 us
  other arithmetic: 1.8 us -> 0.65 us
  Pallas kernels: 2.67 us -> 2.1 us
  starting transfers between devices: 0.57 us -> 0.19 us
    squeeze x3 -> x0, local copies, waits for them, and re-layouts: 2.65 us -> none  [local_by_channels(): lax.dynamic_index_in_dim(t, part, 0, keepdims=False)]
    ppermute x1, waiting for transfers between devices: 0.01 us -> 1.33 us  [local_by_channels(): swapped = lax.ppermute(got, 'col', pairs)]
    dynamic_slice x1 -> x0, local copies, waits for them, and re-layouts: 1.24 us -> none  [local_by_channels(): skip[turn * rows + lax.axis_index('row')]]
    ppermute x1, waiting for transfers between devices: 0.01 us -> 1.22 us  [local_by_channels(): other = lax.ppermute(unwound, 'col', pairs)]
    select_n x1 -> x0, other arithmetic: 1.15 us -> none  [local_by_channels(): jnp.where(jnp.arange(parts) // 2 == part // 2, skip[turn * rows + lax.axi...]
    pallas_call x2 -> x3, Pallas kernels: 1.6 us -> 1.1 us  [call(): pl.pallas_call(kernel, out_shape=pltpu.VMEM(out_shape, kind), in_specs=[p...]
    ppermute x1, starting transfers between devices: 0.57 us -> 0.19 us  [local_by_channels(): other = lax.ppermute(unwound, 'col', pairs)]
  transfers between devices with their start and end apart: 2 -> 2, of which waited for: 0 -> 2; matrix products, arithmetic and copies ran while one was open for 14% -> 0% of each run, Pallas kernels for 0% -> 0%
where the time goes in v3:
time: 34 us; the launch traced here: 33.7 us
  blocking collectives  28.1 us (83%)
  waiting for transfers between devices  2.55 us (7%)
  Pallas kernels  2.1 us (6%)
  other arithmetic  0.65 us (2%)
    all_to_all x1, blocking collectives, local_by_channels(): lax.all_to_all(send.reshape(rows * parts, tall, col_count), every, 0, 0,...  17.7 us
    all_to_all x1, blocking collectives, local_by_channels(): lax.all_to_all(partial_sums.reshape(rows * parts, half, col_count), every...  10.4 us
    ppermute x1, waiting for transfers between devices, local_by_channels(): swapped = lax.ppermute(got, 'col', pairs)  1.33 us
    ppermute x1, waiting for transfers between devices, local_by_channels(): other = lax.ppermute(unwound, 'col', pairs)  1.22 us
    pallas_call x3, Pallas kernels, call(): pl.pallas_call(kernel, out_shape=pltpu.VMEM(out_shape, kind), in_specs=[p...  1.1 us
    pallas_call x1, Pallas kernels, local_by_channels(): pl.pallas_call(pack_kernel, out_shape=pltpu.VMEM((rows, parts, tall, col_...  1 us
  transfers between devices with their start and end apart: 2, of which 2 were waited for; matrix products, arithmetic and copies ran while one was open for 0% of the time, Pallas kernels for 0%

profile of v3, /device:TPU:0, one launch (start us, length us, event | category | flops | bytes accessed | tf_op | source)
XLA Modules:
  0.0 33.7 jit_solution(574339156377193320)
XLA Ops:
  0.0 1.0 %shard_map.91 = bf16[8,4,32,128]{3,2,1,0:T(8,128)(2,1)S(1)} custom-call(bf16[8,32,128]{2,1,0:T(8,128)(2,1)} %signal_ref.1, bf16[8,32,128]{2,1,0:T(8,128)(2,1)} %real_ref.1, bf16[8,32,128]{2,1,0:T(8,128)(2,1)} %imag_ref.1), custom_call_target="tpu_custom_call" | custom-call | tf_op jit(solution)/shard_map/pallas_call | solution.py:229
  1.0 0.0 copy-start.2
  1.0 17.7 %all_to_all.10 = bf16[32,32,128]{2,1,0:T(8,128)(2,1)S(1)} all-to-all(bf16[32,32,128]{2,1,0:T(8,128)(2,1)S(1)} %bitcast.9), channel_id=1, replica_groups=mesh['row'=8,'col'=4] {'row','col'}, dimensions={0} | all-to-all | bytes 524288 | tf_op jit(solution)/shard_map/all_to_all | solution.py:236
  18.7 0.0 copy-start
  18.7 0.0 copy-start.3
  18.7 0.0 copy-start.4
  18.7 0.0 collective-permute-start
  18.7 0.0 copy-done.2
  18.8 0.2 shard_map.92.near_ref
  18.9 0.0 copy-start.1
  18.9 1.3 %collective-permute-done.swapped_ref = bf16[8,4,32,128]{3,2,1,0:T(8,128)(2,1)S(1)} collective-permute-done((bf16[8,4,32,128]{3,2,1,0:T(8,128)(2,1)S(1)}, bf16[8,4,32,128]{3,2,1,0:T(8,128)(2,1)S(1)}, u32[]{:S(2)}, u32[]{:S(2)}) %collective-permute-start) | collective-permute-done | bytes 262176 | tf_op jit(solution)/shard_map/ppermute | solution.py:238
  20.3 0.0 copy-done
  20.3 0.0 copy-done.3
  20.3 0.0 copy-done.4
  20.3 0.7 %shard_map.93.own_ref = bf16[128,512]{1,0:T(8,128)(2,1)S(1)} custom-call(f32[128,512]{1,0:T(8,128)S(1)} %shard_map.92.near_ref, bf16[8,4,32,128]{3,2,1,0:T(8,128)(2,1)S(1)} %bitcast.7, bf16[8,4,32,128]{3,2,1,0:T(8,128)(2,1)S(1)} %collective-permute-done.swapped_ref, bf16[4,128,256]{2,1,0:T(8,128)(2,1)S(1)} %copy-done.2, f32[2,8,512]{2,1,0:T(8,128)S(1)} %copy-done.4, ...), custom_call_target="tpu_custom_call" | custom-call | tf_op jit(solution)/shard_map/pallas_call | solution.py:207
  21.0 0.0 copy-start.5
  21.0 0.2 collective-permute-start.1
  21.2 1.2 %collective-permute-done.1.other_ref = bf16[128,512]{1,0:T(8,128)(2,1)S(1)} collective-permute-done((bf16[128,512]{1,0:T(8,128)(2,1)S(1)}, bf16[128,512]{1,0:T(8,128)(2,1)S(1)}, u32[]{:S(2)}, u32[]{:S(2)}) %collective-permute-start.1) | collective-permute-done | bytes 131104 | tf_op jit(solution)/shard_map/ppermute | solution.py:242
  22.5 0.0 copy-done.1
  22.5 0.0 copy-done.5
  22.5 0.2 shard_map.94
  22.7 10.4 %all_to_all.11 = bf16[32,16,128]{2,1,0:T(8,128)(2,1)S(1)} all-to-all(bf16[32,16,128]{2,1,0:T(8,128)(2,1)S(1)} %bitcast.10), channel_id=1, replica_groups=mesh['row'=8,'col'=4] {'row','col'}, dimensions={0} | all-to-all | bytes 262144 | tf_op jit(solution)/shard_map/all_to_all | solution.py:252
  33.1 0.7 %reduce_sum.12 = bf16[8,32,128]{2,1,0:T(8,128)(2,1)} reduce(bf16[8,2,32,128]{3,2,1,0:T(8,128)(2,1)S(1)} %bitcast.12, bf16[]{:T(256)} %constant.12.clone.1), dimensions={1}, to_apply=%region_0.0 | reduce | flops 32768 | bytes 196610 | tf_op jit(solution)/shard_map/reduce_sum | solution.py:254
Async XLA Ops:
  1.0 17.7 %copy-start.2 = (bf16[4,128,256]{2,1,0:T(8,128)(2,1)S(1)}, bf16[4,128,256]{2,1,0:T(8,128)(2,1)}, u32[]{:S(2)}) copy-start(bf16[4,128,256]{2,1,0:T(8,128)(2,1)} %constant.13.clone.first_ref) | copy-start | bytes 786436
  18.7 1.5 %copy-start = (bf16[512,1024]{1,0:T(8,128)(2,1)S(1)}, bf16[512,1024]{1,0:T(8,128)(2,1)}, u32[]{:S(2)}) copy-start(bf16[512,1024]{1,0:T(8,128)(2,1)} %constant.17.clone.second_ref) | copy-start | bytes 3145732
  18.7 1.5 %copy-start.3 = (f32[4,2,8,512]{3,2,1,0:T(8,128)S(1)}, f32[4,2,8,512]{3,2,1,0:T(8,128)}, u32[]{:S(2)}) copy-start(f32[4,2,8,512]{3,2,1,0:T(8,128)} %constant.15.clone.row_ref) | copy-start | bytes 393220
  18.7 1.5 %copy-start.4 = (f32[2,8,512]{2,1,0:T(8,128)S(1)}, f32[2,8,512]{2,1,0:T(8,128)}, u32[]{:S(2)}) copy-start(f32[2,8,512]{2,1,0:T(8,128)} %constant.14.clone.block_ref) | copy-start | bytes 98308
  18.7 1.5 %collective-permute-start = (bf16[8,4,32,128]{3,2,1,0:T(8,128)(2,1)S(1)}, bf16[8,4,32,128]{3,2,1,0:T(8,128)(2,1)S(1)}, u32[]{:S(2)}, u32[]{:S(2)}) collective-permute-start(bf16[8,4,32,128]{3,2,1,0:T(8,128)(2,1)S(1)} %bitcast.5), channel_id=1, source_target_pairs={{0,1},{1,0},{2,3},{3,2},{4,5},{5,4},{6,7},{7,6},{8,9},{9,8},{10,11... | collective-permute-start | bytes 786440 | tf_op jit(solution)/shard_map/ppermute | solution.py:238
  18.9 3.5 %copy-start.1 = (bf16[4,128,256]{2,1,0:T(8,128)(2,1)S(1)}, bf16[4,128,256]{2,1,0:T(8,128)(2,1)}, u32[]{:S(2)}) copy-start(bf16[4,128,256]{2,1,0:T(8,128)(2,1)} %constant.16.clone.inverse_ref) | copy-start | bytes 786436
  21.0 1.4 %copy-start.5 = (f32[8]{0:T(128)S(1)}, f32[8]{0:T(128)}, u32[]{:S(2)}) copy-start(f32[8]{0:T(128)} %param.12) | copy-start | bytes 100
  21.0 1.4 %collective-permute-start.1 = (bf16[128,512]{1,0:T(8,128)(2,1)S(1)}, bf16[128,512]{1,0:T(8,128)(2,1)S(1)}, u32[]{:S(2)}, u32[]{:S(2)}) collective-permute-start(bf16[128,512]{1,0:T(8,128)(2,1)S(1)} %shard_map.93.own_ref), channel_id=1, source_target_pairs={{0,1},{1,0},{2,3},{3,2},{4,5},{5,4},{6,7},{7,6},{8,9},{9,8},{10,11... | collective-permute-start | bytes 393224 | tf_op jit(solution)/shard_map/ppermute | solution.py:242

commit v4 on v0

--- a/solution.py
+++ b/solution.py
@@ -1,8 +1,12 @@
+import functools
 import math
 
 import jax
 import jax.numpy as jnp
+import numpy as np
 from jax import lax
+from jax.experimental import pallas as pl
+from jax.experimental.pallas import tpu as pltpu
 from jax.sharding import PartitionSpec as P
 
 
@@ -26,7 +30,7 @@
     return jnp.einsum("rn,cnj->crj", phase, series, preferred_element_type=jnp.float32)
 
 
-def local(signal, filter_real, filter_imag, skip):
+def local_by_columns(signal, filter_real, filter_imag, skip):
     channels, row_count, col_count = signal.shape
     first_len = row_count * lax.axis_size("row")
     second_len = col_count * lax.axis_size("col")
@@ -52,26 +56,16 @@
         lax.all_to_all(pair_mix_re, "row", split_axis=1, concat_axis=2, tiled=True),
         lax.all_to_all(pair_mix_im, "row", split_axis=1, concat_axis=2, tiled=True),
     )
-    pieces = (
-        lax.all_gather(mixed_re, "col", axis=2, tiled=True),
-        lax.all_gather(mixed_im, "col", axis=2, tiled=True),
-    )
-    amount = pieces[0].shape[2]
-    phase_re, phase_im = phase_table(jnp.arange(amount, dtype=jnp.int32), own_cols, second_len)
-    part_re, part_im = pieces
-    new_re = column_product(part_re, phase_re) - column_product(part_im, phase_im)
-    new_im = column_product(part_re, phase_im) + column_product(part_im, phase_re)
-    spec_re = new_re
-    spec_im = new_im
+    part_re = lax.all_gather(mixed_re, "col", axis=2, tiled=True)
+    part_im = lax.all_gather(mixed_im, "col", axis=2, tiled=True)
+    all_cols = jnp.arange(second_len, dtype=jnp.int32)
+    phase_re, phase_im = phase_table(all_cols, own_cols, second_len)
+    spec_re = column_product(part_re, phase_re) - column_product(part_im, phase_im)
+    spec_im = column_product(part_re, phase_im) + column_product(part_im, phase_re)
     prod_re = (spec_re * filter_real - spec_im * filter_imag).astype(jnp.bfloat16)
     prod_im = (spec_re * filter_imag + spec_im * filter_real).astype(jnp.bfloat16)
-    pieces = (
-        lax.all_gather(prod_re, "col", axis=2, tiled=True),
-        lax.all_gather(prod_im, "col", axis=2, tiled=True),
-    )
-    amount = pieces[0].shape[2]
-    phase_re, phase_im = phase_table(jnp.arange(amount, dtype=jnp.int32), own_cols, second_len)
-    part_re, part_im = pieces
+    part_re = lax.all_gather(prod_re, "col", axis=2, tiled=True)
+    part_im = lax.all_gather(prod_im, "col", axis=2, tiled=True)
     new_re = column_product(part_re, phase_re) + column_product(part_im, phase_im)
     new_im = column_product(part_im, phase_re) - column_product(part_re, phase_im)
     unwound_re = (new_re * twist_re + new_im * twist_im).astype(jnp.bfloat16)
@@ -87,6 +81,277 @@
     return lax.all_to_all(pair_out, "row", split_axis=1, concat_axis=2, tiled=True)
 
 
+def numpy_phase(left_ids, right_ids, modulus):
+    product = (left_ids[:, None].astype(np.int64) * right_ids[None, :]) % modulus
+    angle = np.float32(-2.0 * math.pi / modulus) * product.astype(np.float32)
+    return np.cos(angle), np.sin(angle)
+
+
+def tables(first_len, second_len, row_count, parts):
+    height = row_count // parts
+    rows = np.arange(first_len)
+    cols = np.arange(second_len)
+    by_core = cols.reshape(parts, 2, -1).swapaxes(0, 1).reshape(-1)
+    blocks = rows.reshape(-1, row_count)
+    own = [blocks[:, part * height : (part + 1) * height].reshape(-1) for part in range(parts)]
+    first = np.stack(numpy_phase(rows, rows, first_len))
+    sides = [[[kind[own[2 * side + core]] for core in range(2)] for kind in first] for side in range(parts // 2)]
+    inverse = [
+        np.concatenate([kind[:, own[member]] for kind in first for member in (part, part ^ 1)], axis=1)
+        for part in range(parts)
+    ]
+    block_twist = numpy_phase(blocks[:, 0], by_core, first_len * second_len)
+    row_twist = numpy_phase(blocks[0], by_core, first_len * second_len)
+    forward = np.concatenate(numpy_phase(by_core, cols, second_len), axis=1)
+    backward = np.concatenate(numpy_phase(cols, by_core, second_len), axis=1)
+    return (
+        jnp.asarray(np.array(sides), jnp.bfloat16),
+        jnp.asarray(np.stack(block_twist), jnp.float32),
+        jnp.asarray(np.stack(row_twist), jnp.float32),
+        jnp.asarray(np.stack(inverse), jnp.bfloat16),
+        jnp.asarray(forward, jnp.bfloat16),
+        jnp.asarray(backward, jnp.bfloat16),
+    )
+
+
+def dot(left, right):
+    return jnp.dot(left, right, preferred_element_type=jnp.float32)
+
+
+def crossed(one, two):
+    half = one.shape[-1] // 2
+    return (
+        jnp.concatenate([one[..., :half], two[..., :half]], axis=-1),
+        jnp.concatenate([one[..., half:], two[..., half:]], axis=-1),
+    )
+
+
+def side_and_core():
+    part = lax.axis_index("col")
+    return part // 2, part % 2
+
+
+def half_of(core, width):
+    return pl.ds(pl.multiple_of(core * width, width), width)
+
+
+def series_of(ref):
+    rows, parts, tall, width = ref.shape
+    half = tall // 2
+    strips = []
+    for part in range(0, parts, 2):
+        pair = crossed(ref[:, part, :half, :], ref[:, part + 1, :half, :])
+        strips.append(jnp.concatenate(pair, axis=1).reshape(rows * 2 * half, width))
+    return jnp.concatenate(strips, axis=1)
+
+
+def filter_of(ref, start, count):
+    rows, parts, _, width = ref.shape
+    return jnp.concatenate(
+        [ref[:, part, start : start + count, :].astype(jnp.float32).reshape(rows * count, width) for part in range(parts)],
+        axis=1,
+    )
+
+
+def twists(block_ref, row_ref, height, side, core, span):
+    block_re, block_im = block_ref[0, :, span][:, None, :], block_ref[1, :, span][:, None, :]
+    shape = (block_ref.shape[1] * height, span.size)
+    re, im = [], []
+    for member in (core, 1 - core):
+        at = pl.ds(pl.multiple_of((2 * side + member) * height, height), height)
+        row_re, row_im = row_ref[0, at, span][None], row_ref[1, at, span][None]
+        re.append((block_re * row_re - block_im * row_im).reshape(shape))
+        im.append((block_re * row_im + block_im * row_re).reshape(shape))
+    return jnp.concatenate(re, axis=0), jnp.concatenate(im, axis=0)
+
+
+def turned(re, im, by_re, by_im):
+    return re * by_re - im * by_im, re * by_im + im * by_re
+
+
+def widened(pair):
+    re, im = (each.astype(jnp.bfloat16) for each in pair)
+    return jnp.concatenate([jnp.concatenate([re, -im], axis=1), jnp.concatenate([im, re], axis=1)], axis=0)
+
+
+def widened_back(pair):
+    re, im = (each.astype(jnp.bfloat16) for each in pair)
+    return jnp.concatenate([jnp.concatenate([re, im], axis=1), jnp.concatenate([im, -re], axis=1)], axis=0)
+
+
+def pack_kernel(signal_ref, real_ref, imag_ref, skip_ref, send_ref, skips_ref, signal_buf, sems):
+    _, parts, _, _ = send_ref.shape
+    row_count = signal_ref.shape[-2]
+    half = row_count // 2
+    height = row_count // parts
+    copies = [(signal_ref, signal_buf), (skip_ref, skips_ref)]
+    for part in range(parts):
+        cut = slice(part * height, (part + 1) * height)
+        copies.append((real_ref.at[:, cut], send_ref.at[:, part, half : half + height]))
+        copies.append((imag_ref.at[:, cut], send_ref.at[:, part, half + height :]))
+    copies = [pltpu.make_async_copy(a, b, sems.at[i]) for i, (a, b) in enumerate(copies)]
+    for copy in copies:
+        copy.start()
+    copies[0].wait()
+    halves = crossed(signal_buf[:, :half], signal_buf[:, half:])
+    for part in range(parts):
+        send_ref[:, part, :half] = halves[part % 2]
+    for copy in copies[1:]:
+        copy.wait()
+
+
+def half_transform(ref, first_ref, side, core):
+    left = [first_ref[side, kind, member] for kind in range(2) for member in (core, 1 - core)]
+    both = dot(jnp.concatenate(left, axis=0), series_of(ref))
+    mine = both.shape[0] // 2
+    return both[:mine], both[mine:]
+
+
+def forward_rows(forward_ref, core):
+    second_len = forward_ref.shape[0]
+    rows = half_of(core, second_len // 2)
+    return jnp.concatenate([forward_ref[rows, :second_len], forward_ref[rows, second_len:]], axis=0)
+
+
+def near_kernel(got_ref, first_ref, block_ref, row_ref, forward_ref, skip_ref, spec_ref, twist_ref, term_ref, *, turn):
+    rows, parts, tall, width = got_ref.shape
+    side, core = side_and_core()
+    first_len, second_len = first_ref.shape[-1], forward_ref.shape[0]
+    height = tall // 4
+    near_len = second_len // 2
+    twist = twists(block_ref, row_ref, height, side, core, half_of(core, near_len))
+    mixed = turned(*half_transform(got_ref, first_ref, side, core), *twist)
+    spec_ref[...] = dot(widened(mixed), forward_rows(forward_ref, core))
+    twist_ref[0], twist_ref[1] = twists(block_ref, row_ref, height, side, core, half_of(1 - core, near_len))
+    twist_ref[2], twist_ref[3] = (each / (first_len * second_len) for each in twist)
+
+    at = lax.broadcasted_iota(jnp.int32, skip_ref.shape, 1)
+    channel = turn * rows + lax.axis_index("row")
+    skip = jnp.sum(jnp.where(at == channel, skip_ref[...], 0.0), axis=1, keepdims=True)
+    series = series_of(got_ref)
+    for place in range(parts // 2):
+        cut = slice(place * width, (place + 1) * width)
+        term_ref[:, cut] = jnp.where(side == place, skip, 0.0) * series[:, cut].astype(jnp.float32)
+
+
+def spectrum_kernel(spec_ref, twist_ref, term_ref, got_ref, swapped_ref, first_ref, forward_ref, backward_ref, inverse_ref, out_ref):
+    rows, parts, tall, width = got_ref.shape
+    side, core = side_and_core()
+    half, height = tall // 2, tall // 4
+    second_len = forward_ref.shape[0]
+    near_len = second_len // 2
+    mixed = turned(*half_transform(swapped_ref, first_ref, side, core), twist_ref[0], twist_ref[1])
+    spec = spec_ref[...] + dot(widened(mixed), forward_rows(forward_ref, 1 - core))
+    mine = spec.shape[0] // 2
+    filt_re, filt_im = (
+        jnp.concatenate([filter_of(ref, start, height) for ref in (got_ref, swapped_ref)], axis=0)
+        for start in (half, half + height)
+    )
+    prod = turned(spec[:mine], spec[mine:], filt_re, filt_im)
+    cols = [pl.ds(pl.multiple_of(at + core * near_len, near_len), near_len) for at in (0, second_len)]
+    back = dot(widened_back(prod), jnp.concatenate([backward_ref[:, col] for col in cols], axis=0))
+    unwound = turned(back[:mine], back[mine:], twist_ref[2], -twist_ref[3])
+    unwound = jnp.concatenate(unwound, axis=0).astype(jnp.bfloat16)
+    total = (dot(inverse_ref[lax.axis_index("col")], unwound) + term_ref[...]).astype(jnp.bfloat16)
+    for place in range(parts // 2):
+        piece = total[:, place * width : (place + 1) * width].reshape(rows, 2 * half, width)
+        out_ref[:, 2 * place], out_ref[:, 2 * place + 1] = crossed(piece[:, :half], piece[:, half:])
+
+
+def finish_kernel(back_ref, out_ref):
+    _, parts, half, _ = back_ref.shape
+    cores = []
+    for core in range(2):
+        shares = [back_ref[:, part].astype(jnp.float32) for part in range(core, parts, 2)]
+        cores.append(sum(shares[1:], shares[0]))
+    out_ref[:, :half], out_ref[:, half:] = (each.astype(jnp.bfloat16) for each in crossed(*cores))
+
+
+PARAMS = pltpu.CompilerParams(vmem_limit_bytes=8 * 2**20)
+IN_VMEM = pl.BlockSpec(memory_space=pltpu.VMEM)
+
+
+def call(kernel, outs, *args, flops=None):
+    return pl.pallas_call(
+        kernel,
+        out_shape=[pltpu.VMEM(shape, kind) for shape, kind in outs],
+        in_specs=[IN_VMEM] * len(args),
+        out_specs=[IN_VMEM] * len(outs),
+        compiler_params=PARAMS,
+        cost_estimate=flops and pl.CostEstimate(flops=flops, bytes_accessed=0, transcendentals=0),
+    )(*(pltpu.with_memory_space_constraint(arg, pltpu.VMEM) for arg in args))
+
+
+def local_by_channels(signal, filter_real, filter_imag, skip):
+    channels, row_count, col_count = signal.shape
+    rows = lax.axis_size("row")
+    parts = lax.axis_size("col")
+    share = channels // rows
+    half = row_count // 2
+    pairs = [(part, part ^ 1) for part in range(parts)]
+    first, block, row, inverse, forward, backward = tables(rows * row_count, parts * col_count, row_count, parts)
+    near_len = parts * col_count // 2
+    mine = rows * row_count // (parts // 2)
+    outs = []
+
+    def exchange(array):
+        flat = array.reshape((rows * parts,) + array.shape[2:])
+        return lax.all_to_all(flat, ("row", "col"), 0, 0, tiled=True).reshape(array.shape)
+
+    for turn in range(share):
+        own = slice(turn * rows, (turn + 1) * rows)
+        tall = half + 2 * (row_count // parts)
+        args = (signal[own], filter_real[own], filter_imag[own], skip[None])
+        send, skips = pl.pallas_call(
+            pack_kernel,
+            out_shape=[pltpu.VMEM((rows, parts, tall, col_count), jnp.bfloat16), pltpu.VMEM((1, channels), jnp.float32)],
+            in_specs=[pl.BlockSpec(memory_space=pltpu.HBM)] * len(args),
+            out_specs=[IN_VMEM] * 2,
+            scratch_shapes=[
+                pltpu.VMEM((rows, row_count, col_count), jnp.bfloat16),
+                pltpu.SemaphoreType.DMA((2 * parts + 2,)),
+            ],
+            compiler_params=PARAMS,
+            cost_estimate=pl.CostEstimate(flops=10**9, bytes_accessed=0, transcendentals=0),
+        )(*(pltpu.with_memory_space_constraint(arg, pltpu.HBM) for arg in args))
+        got = exchange(send)
+        swapped = lax.ppermute(got, "col", pairs)
+        near = call(
+            functools.partial(near_kernel, turn=turn),
+            [
+                ((2 * mine, 2 * near_len), jnp.float32),
+                ((4, mine, near_len), jnp.float32),
+                ((rows * row_count, near_len), jnp.float32),
+            ],
+            *(got, first, block, row, forward, skips),
+            flops=10**9,
+        )
+        (partial_sums,) = call(
+            spectrum_kernel,
+            [((rows, parts, half, col_count), jnp.bfloat16)],
+            *(*near, got, swapped, first, forward, backward, inverse),
+        )
+        back = exchange(partial_sums)
+        outs.append(
+            pl.pallas_call(
+                finish_kernel,
+                out_shape=jax.ShapeDtypeStruct((rows, row_count, col_count), jnp.bfloat16),
+                in_specs=[IN_VMEM],
+                compiler_params=PARAMS,
+            )(pltpu.with_memory_space_constraint(back, pltpu.VMEM))
+        )
+    return outs[0] if share == 1 else jnp.concatenate(outs, axis=0)
+
+
+def local(signal, filter_real, filter_imag, skip):
+    channels, row_count, col_count = signal.shape
+    parts = lax.axis_size("col")
+    fits = parts % 2 == 0 and row_count == 8 * parts and col_count % 128 == 0
+    if channels % lax.axis_size("row") == 0 and fits:
+        return local_by_channels(signal, filter_real, filter_imag, skip)
+    return local_by_columns(signal, filter_real, filter_imag, skip)
+
+
 def solution(mesh):
     in_specs = (P(None, "row", "col"), P(None, "row", "col"), P(None, "row", "col"), P())
     out_specs = P(None, "row", "col")

time: 108 us -> 32.9 us (0.30)
  starting transfers between devices: 23.3 us -> 0.01 us
  waiting for transfers between devices: 24 us -> 0.97 us
  matrix products: 13.7 us -> 0 us
  local copies, waits for them, and re-layouts: 12.9 us -> 0.04 us
  blocking collectives: 33 us -> 28.1 us
  Pallas kernels: 0 us -> 3.54 us
    all_to_all x5 -> x0, waiting for transfers between devices: 24 us -> none  [the longest x1 6.72 us: local(): lax.all_to_all(signal, 'row', split_axis=2, concat_axis=1, tiled=True)]
    all_gather x4 -> x0, blocking collectives: 23.7 us -> none  [the longest x1 6.09 us: local(): lax.all_gather(prod_re, 'col', axis=2, tiled=True)]
    all_to_all x5 -> x0, starting transfers between devices: 23.3 us -> none  [the longest x1 7.31 us: local(): lax.all_to_all(signal, 'row', split_axis=2, concat_axis=1, tiled=True)]
    all_to_all x1 -> x2, blocking collectives: 9.29 us -> 28.1 us  [exchange(): lax.all_to_all(flat, ('row', 'col'), 0, 0, tiled=True).reshape(array.shape)]
    dot_general x10 -> x0, matrix products: 11.5 us -> none  [the longest x8 9.28 us: column_product(): jnp.einsum('crn,nk->crk', series, phase, preferred_element_type=jnp.float32)]
    unnamed x19 -> x12, local copies, waits for them, and re-layouts: 8.34 us -> 0.04 us
    pallas_call x0 -> x4, Pallas kernels: none -> 3.54 us  [the longest x2 1.71 us: call(): pl.pallas_call(kernel, out_shape=[pltpu.VMEM(shape, kind) for shape, kind...]
    all_to_all x12 -> x0, local copies, waits for them, and re-layouts: 3.24 us -> none  [the longest x2 1.14 us: local(): lax.all_to_all(pair_out, 'row', split_axis=1, concat_axis=2, tiled=True)]
  transfers between devices with their start and end apart: 5 -> 1, of which waited for: 4 -> 1; matrix products, arithmetic and copies ran while one was open for 6% -> 0% of each run, Pallas kernels for 0% -> 2%
where the time goes in v4:
time: 32.9 us; the launch traced here: 32.7 us
  blocking collectives  28.1 us (85%)
  Pallas kernels  3.54 us (11%)
  waiting for transfers between devices  0.97 us (3%)
    all_to_all x2, blocking collectives, exchange(): lax.all_to_all(flat, ('row', 'col'), 0, 0, tiled=True).reshape(array.shape)  28.1 us
    pallas_call x2, Pallas kernels, call(): pl.pallas_call(kernel, out_shape=[pltpu.VMEM(shape, kind) for shape, kind...  1.71 us
    pallas_call x1, Pallas kernels, local_by_channels(): pl.pallas_call(pack_kernel, out_shape=[pltpu.VMEM((rows, parts, tall, col...  1.12 us
    ppermute x1, waiting for transfers between devices, local_by_channels(): swapped = lax.ppermute(got, 'col', pairs)  0.97 us
    pallas_call x1, Pallas kernels, local_by_channels(): pl.pallas_call(finish_kernel, out_shape=jax.ShapeDtypeStruct((rows, row_c...  0.72 us
  transfers between devices with their start and end apart: 1, of which 1 were waited for; matrix products, arithmetic and copies ran while one was open for 0% of the time, Pallas kernels for 2%

profile of v4, /device:TPU:0, one launch (start us, length us, event | category | flops | bytes accessed | tf_op | source)
XLA Modules:
  0.0 32.7 jit_solution(11281969062346729021)
XLA Ops:
  0.0 0.0 copy-start
  0.0 1.1 %shard_map.100 = (bf16[8,4,32,128]{3,2,1,0:T(8,128)(2,1)S(1)}, f32[1,8]{1,0:T(1,128)S(1)}) custom-call(bf16[8,32,128]{2,1,0:T(8,128)(2,1)} %signal_ref.1, bf16[8,32,128]{2,1,0:T(8,128)(2,1)} %real_ref.1, bf16[8,32,128]{2,1,0:T(8,128)(2,1)} %imag_ref.1, f32[1,8]{1,0:T(1,128)} %bitcast.11), custom_call_target="tpu_custom_call" | custom-call | flops 1000000000 | tf_op jit(solution)/shard_map/pallas_call | solution.py:305
  1.1 0.0 copy-start.3
  1.1 0.0 copy-start.4
  1.2 0.0 copy-start.5
  1.2 17.7 %all_to_all.10 = bf16[32,32,128]{2,1,0:T(8,128)(2,1)S(1)} all-to-all(bf16[32,32,128]{2,1,0:T(8,128)(2,1)S(1)} %bitcast.10), channel_id=1, replica_groups=mesh['row'=8,'col'=4] {'row','col'}, dimensions={0} | all-to-all | bytes 524288 | tf_op jit(solution)/shard_map/all_to_all | solution.py:299
  18.9 0.0 collective-permute-start
  18.9 0.0 copy-done
  18.9 0.0 copy-done.3
  18.9 0.0 copy-done.4
  18.9 0.0 copy-done.5
  18.9 0.0 copy-start.1
  18.9 0.0 copy-start.2
  18.9 0.5 %shard_map.101 = (f32[256,512]{1,0:T(8,128)S(1)}, f32[4,128,256]{2,1,0:T(8,128)S(1)}, f32[256,256]{1,0:T(8,128)S(1)}) custom-call(bf16[8,4,32,128]{3,2,1,0:T(8,128)(2,1)S(1)} %bitcast.6, bf16[2,2,2,64,256]{4,3,2,1,0:T(8,128)(2,1)S(1)} %copy-done.3, f32[2,8,512]{2,1,0:T(8,128)S(1)} %copy-done.5, f32[2,32,512]{2,1,0:T(8,128)S(1)} %copy-done.4, ...), custom_call_target="tpu_custom_call" | custom-call | flops 1000000000 | tf_op jit(solution)/shard_map/pallas_call | solution.py:275
  19.4 1.0 %collective-permute-done.swapped_ref = bf16[8,4,32,128]{3,2,1,0:T(8,128)(2,1)S(1)} collective-permute-done((bf16[8,4,32,128]{3,2,1,0:T(8,128)(2,1)S(1)}, bf16[8,4,32,128]{3,2,1,0:T(8,128)(2,1)S(1)}, u32[]{:S(2)}, u32[]{:S(2)}) %collective-permute-start) | collective-permute-done | bytes 262176 | tf_op jit(solution)/shard_map/ppermute | solution.py:318
  20.4 0.0 copy-done.1
  20.4 0.0 copy-done.2
  20.4 1.2 %shard_map.102 = bf16[8,4,16,128]{3,2,1,0:T(8,128)(2,1)S(1)} custom-call(f32[256,512]{1,0:T(8,128)S(1)} %get-tuple-element.12.spec_ref, f32[4,128,256]{2,1,0:T(8,128)S(1)} %get-tuple-element.13.twist_ref, f32[256,256]{1,0:T(8,128)S(1)} %get-tuple-element.14.term_ref, bf16[8,4,32,128]{3,2,1,0:T(8,128)(2,1)S(1)} %bitcast.7, ...), custom_call_target="tpu_custom_call" | custom-call | tf_op jit(solution)/shard_map/pallas_call | solution.py:275
  21.6 10.4 %all_to_all.11 = bf16[32,16,128]{2,1,0:T(8,128)(2,1)S(1)} all-to-all(bf16[32,16,128]{2,1,0:T(8,128)(2,1)S(1)} %bitcast.8), channel_id=1, replica_groups=mesh['row'=8,'col'=4] {'row','col'}, dimensions={0} | all-to-all | bytes 262144 | tf_op jit(solution)/shard_map/all_to_all | solution.py:299
  32.0 0.7 %shard_map.103 = bf16[8,32,128]{2,1,0:T(8,128)(2,1)} custom-call(bf16[8,4,16,128]{3,2,1,0:T(8,128)(2,1)S(1)} %bitcast.9), custom_call_target="tpu_custom_call" | custom-call | tf_op jit(solution)/shard_map/pallas_call | solution.py:336
Async XLA Ops:
  0.0 18.9 %copy-start = (bf16[512,1024]{1,0:T(8,128)(2,1)S(1)}, bf16[512,1024]{1,0:T(8,128)(2,1)}, u32[]{:S(2)}) copy-start(bf16[512,1024]{1,0:T(8,128)(2,1)} %constant.16.clone.forward_ref) | copy-start | bytes 3145732
  1.1 17.8 %copy-start.3 = (bf16[2,2,2,64,256]{4,3,2,1,0:T(8,128)(2,1)S(1)}, bf16[2,2,2,64,256]{4,3,2,1,0:T(8,128)(2,1)}, u32[]{:S(2)}) copy-start(bf16[2,2,2,64,256]{4,3,2,1,0:T(8,128)(2,1)} %constant.12.clone.first_ref) | copy-start | bytes 786436
  1.1 17.7 %copy-start.4 = (f32[2,32,512]{2,1,0:T(8,128)S(1)}, f32[2,32,512]{2,1,0:T(8,128)}, u32[]{:S(2)}) copy-start(f32[2,32,512]{2,1,0:T(8,128)} %constant.14.clone.row_ref) | copy-start | bytes 393220
  1.2 17.7 %copy-start.5 = (f32[2,8,512]{2,1,0:T(8,128)S(1)}, f32[2,8,512]{2,1,0:T(8,128)}, u32[]{:S(2)}) copy-start(f32[2,8,512]{2,1,0:T(8,128)} %constant.13.clone.block_ref) | copy-start | bytes 98308
  18.9 1.5 %collective-permute-start = (bf16[8,4,32,128]{3,2,1,0:T(8,128)(2,1)S(1)}, bf16[8,4,32,128]{3,2,1,0:T(8,128)(2,1)S(1)}, u32[]{:S(2)}, u32[]{:S(2)}) collective-permute-start(bf16[8,4,32,128]{3,2,1,0:T(8,128)(2,1)S(1)} %bitcast.5), channel_id=1, source_target_pairs={{0,1},{1,0},{2,3},{3,2},{4,5},{5,4},{6,7},{7,6},{8,9},{9,8},{10,11... | collective-permute-start | bytes 786440 | tf_op jit(solution)/shard_map/ppermute | solution.py:318
  18.9 1.5 %copy-start.1 = (bf16[512,1024]{1,0:T(8,128)(2,1)S(1)}, bf16[512,1024]{1,0:T(8,128)(2,1)}, u32[]{:S(2)}) copy-start(bf16[512,1024]{1,0:T(8,128)(2,1)} %constant.17.clone.backward_ref) | copy-start | bytes 3145732
  18.9 1.5 %copy-start.2 = (bf16[4,256,256]{2,1,0:T(8,128)(2,1)S(1)}, bf16[4,256,256]{2,1,0:T(8,128)(2,1)}, u32[]{:S(2)}) copy-start(bf16[4,256,256]{2,1,0:T(8,128)(2,1)} %constant.15.clone.inverse_ref) | copy-start | bytes 1572868

commit v5 on v4

--- a/solution.py
+++ b/solution.py
@@ -81,6 +81,10 @@
     return lax.all_to_all(pair_out, "row", split_axis=1, concat_axis=2, tiled=True)
 
 
+def row_group(side, member, parts):
+    return side + member * (parts - 1 - 2 * side)
+
+
 def numpy_phase(left_ids, right_ids, modulus):
     product = (left_ids[:, None].astype(np.int64) * right_ids[None, :]) % modulus
     angle = np.float32(-2.0 * math.pi / modulus) * product.astype(np.float32)
@@ -93,7 +97,8 @@
     cols = np.arange(second_len)
     by_core = cols.reshape(parts, 2, -1).swapaxes(0, 1).reshape(-1)
     blocks = rows.reshape(-1, row_count)
-    own = [blocks[:, part * height : (part + 1) * height].reshape(-1) for part in range(parts)]
+    groups = [row_group(part // 2, part % 2, parts) for part in range(parts)]
+    own = [blocks[:, group * height : (group + 1) * height].reshape(-1) for group in groups]
     first = np.stack(numpy_phase(rows, rows, first_len))
     sides = [[[kind[own[2 * side + core]] for core in range(2)] for kind in first] for side in range(parts // 2)]
     inverse = [
@@ -158,7 +163,8 @@
     shape = (block_ref.shape[1] * height, span.size)
     re, im = [], []
     for member in (core, 1 - core):
-        at = pl.ds(pl.multiple_of((2 * side + member) * height, height), height)
+        group = row_group(side, member, row_ref.shape[1] // height)
+        at = pl.ds(pl.multiple_of(group * height, height), height)
         row_re, row_im = row_ref[0, at, span][None], row_ref[1, at, span][None]
         re.append((block_re * row_re - block_im * row_im).reshape(shape))
         im.append((block_re * row_im + block_im * row_re).reshape(shape))
@@ -186,7 +192,8 @@
     height = row_count // parts
     copies = [(signal_ref, signal_buf), (skip_ref, skips_ref)]
     for part in range(parts):
-        cut = slice(part * height, (part + 1) * height)
+        group = row_group(part // 2, part % 2, parts)
+        cut = slice(group * height, (group + 1) * height)
         copies.append((real_ref.at[:, cut], send_ref.at[:, part, half : half + height]))
         copies.append((imag_ref.at[:, cut], send_ref.at[:, part, half + height :]))
     copies = [pltpu.make_async_copy(a, b, sems.at[i]) for i, (a, b) in enumerate(copies)]

time: 32.9 us -> 32.9 us (level)
  no operation moved by 1% of the time
where the time goes in v5:
time: 32.9 us; the launch traced here: 32.7 us
  blocking collectives  28.1 us (85%)
  Pallas kernels  3.56 us (11%)
  waiting for transfers between devices  0.95 us (3%)
    all_to_all x2, blocking collectives, exchange(): lax.all_to_all(flat, ('row', 'col'), 0, 0, tiled=True).reshape(array.shape)  28.1 us
    pallas_call x2, Pallas kernels, call(): pl.pallas_call(kernel, out_shape=[pltpu.VMEM(shape, kind) for shape, kind...  1.72 us
    pallas_call x1, Pallas kernels, local_by_channels(): pl.pallas_call(pack_kernel, out_shape=[pltpu.VMEM((rows, parts, tall, col...  1.12 us
    ppermute x1, waiting for transfers between devices, local_by_channels(): swapped = lax.ppermute(got, 'col', pairs)  0.95 us
    pallas_call x1, Pallas kernels, local_by_channels(): pl.pallas_call(finish_kernel, out_shape=jax.ShapeDtypeStruct((rows, row_c...  0.72 us
  transfers between devices with their start and end apart: 1, of which 1 were waited for; matrix products, arithmetic and copies ran while one was open for 0% of the time, Pallas kernels for 2%

profile of v5, /device:TPU:0, one launch (start us, length us, event | category | flops | bytes accessed | tf_op | source)
XLA Modules:
  0.0 32.7 jit_solution(8303212309973984177)
XLA Ops:
  0.0 0.0 copy-start
  0.0 1.1 %shard_map.100 = (bf16[8,4,32,128]{3,2,1,0:T(8,128)(2,1)S(1)}, f32[1,8]{1,0:T(1,128)S(1)}) custom-call(bf16[8,32,128]{2,1,0:T(8,128)(2,1)} %signal_ref.1, bf16[8,32,128]{2,1,0:T(8,128)(2,1)} %real_ref.1, bf16[8,32,128]{2,1,0:T(8,128)(2,1)} %imag_ref.1, f32[1,8]{1,0:T(1,128)} %bitcast.11), custom_call_target="tpu_custom_call" | custom-call | flops 1000000000 | tf_op jit(solution)/shard_map/pallas_call | solution.py:312
  1.1 0.0 copy-start.3
  1.1 0.0 copy-start.4
  1.2 0.0 copy-start.5
  1.2 17.7 %all_to_all.10 = bf16[32,32,128]{2,1,0:T(8,128)(2,1)S(1)} all-to-all(bf16[32,32,128]{2,1,0:T(8,128)(2,1)S(1)} %bitcast.10), channel_id=1, replica_groups=mesh['row'=8,'col'=4] {'row','col'}, dimensions={0} | all-to-all | bytes 524288 | tf_op jit(solution)/shard_map/all_to_all | solution.py:306
  18.9 0.0 collective-permute-start
  18.9 0.0 copy-done
  18.9 0.0 copy-done.3
  18.9 0.0 copy-done.4
  18.9 0.0 copy-done.5
  18.9 0.0 copy-start.1
  18.9 0.0 copy-start.2
  18.9 0.5 %shard_map.101 = (f32[256,512]{1,0:T(8,128)S(1)}, f32[4,128,256]{2,1,0:T(8,128)S(1)}, f32[256,256]{1,0:T(8,128)S(1)}) custom-call(bf16[8,4,32,128]{3,2,1,0:T(8,128)(2,1)S(1)} %bitcast.6, bf16[2,2,2,64,256]{4,3,2,1,0:T(8,128)(2,1)S(1)} %copy-done.3, f32[2,8,512]{2,1,0:T(8,128)S(1)} %copy-done.5, f32[2,32,512]{2,1,0:T(8,128)S(1)} %copy-done.4, ...), custom_call_target="tpu_custom_call" | custom-call | flops 1000000000 | tf_op jit(solution)/shard_map/pallas_call | solution.py:282
  19.5 0.9 %collective-permute-done.swapped_ref = bf16[8,4,32,128]{3,2,1,0:T(8,128)(2,1)S(1)} collective-permute-done((bf16[8,4,32,128]{3,2,1,0:T(8,128)(2,1)S(1)}, bf16[8,4,32,128]{3,2,1,0:T(8,128)(2,1)S(1)}, u32[]{:S(2)}, u32[]{:S(2)}) %collective-permute-start) | collective-permute-done | bytes 262176 | tf_op jit(solution)/shard_map/ppermute | solution.py:325
  20.4 0.0 copy-done.1
  20.4 0.0 copy-done.2
  20.4 1.2 %shard_map.102 = bf16[8,4,16,128]{3,2,1,0:T(8,128)(2,1)S(1)} custom-call(f32[256,512]{1,0:T(8,128)S(1)} %get-tuple-element.12.spec_ref, f32[4,128,256]{2,1,0:T(8,128)S(1)} %get-tuple-element.13.twist_ref, f32[256,256]{1,0:T(8,128)S(1)} %get-tuple-element.14.term_ref, bf16[8,4,32,128]{3,2,1,0:T(8,128)(2,1)S(1)} %bitcast.7, ...), custom_call_target="tpu_custom_call" | custom-call | tf_op jit(solution)/shard_map/pallas_call | solution.py:282
  21.6 10.4 %all_to_all.11 = bf16[32,16,128]{2,1,0:T(8,128)(2,1)S(1)} all-to-all(bf16[32,16,128]{2,1,0:T(8,128)(2,1)S(1)} %bitcast.8), channel_id=1, replica_groups=mesh['row'=8,'col'=4] {'row','col'}, dimensions={0} | all-to-all | bytes 262144 | tf_op jit(solution)/shard_map/all_to_all | solution.py:306
  32.0 0.7 %shard_map.103 = bf16[8,32,128]{2,1,0:T(8,128)(2,1)} custom-call(bf16[8,4,16,128]{3,2,1,0:T(8,128)(2,1)S(1)} %bitcast.9), custom_call_target="tpu_custom_call" | custom-call | tf_op jit(solution)/shard_map/pallas_call | solution.py:343
Async XLA Ops:
  0.0 18.9 %copy-start = (bf16[512,1024]{1,0:T(8,128)(2,1)S(1)}, bf16[512,1024]{1,0:T(8,128)(2,1)}, u32[]{:S(2)}) copy-start(bf16[512,1024]{1,0:T(8,128)(2,1)} %constant.16.clone.forward_ref) | copy-start | bytes 3145732
  1.1 17.8 %copy-start.3 = (bf16[2,2,2,64,256]{4,3,2,1,0:T(8,128)(2,1)S(1)}, bf16[2,2,2,64,256]{4,3,2,1,0:T(8,128)(2,1)}, u32[]{:S(2)}) copy-start(bf16[2,2,2,64,256]{4,3,2,1,0:T(8,128)(2,1)} %constant.12.clone.first_ref) | copy-start | bytes 786436
  1.1 17.7 %copy-start.4 = (f32[2,32,512]{2,1,0:T(8,128)S(1)}, f32[2,32,512]{2,1,0:T(8,128)}, u32[]{:S(2)}) copy-start(f32[2,32,512]{2,1,0:T(8,128)} %constant.14.clone.row_ref) | copy-start | bytes 393220
  1.2 17.7 %copy-start.5 = (f32[2,8,512]{2,1,0:T(8,128)S(1)}, f32[2,8,512]{2,1,0:T(8,128)}, u32[]{:S(2)}) copy-start(f32[2,8,512]{2,1,0:T(8,128)} %constant.13.clone.block_ref) | copy-start | bytes 98308
  18.9 1.5 %collective-permute-start = (bf16[8,4,32,128]{3,2,1,0:T(8,128)(2,1)S(1)}, bf16[8,4,32,128]{3,2,1,0:T(8,128)(2,1)S(1)}, u32[]{:S(2)}, u32[]{:S(2)}) collective-permute-start(bf16[8,4,32,128]{3,2,1,0:T(8,128)(2,1)S(1)} %bitcast.5), channel_id=1, source_target_pairs={{0,1},{1,0},{2,3},{3,2},{4,5},{5,4},{6,7},{7,6},{8,9},{9,8},{10,11... | collective-permute-start | bytes 786440 | tf_op jit(solution)/shard_map/ppermute | solution.py:325
  18.9 1.5 %copy-start.1 = (bf16[512,1024]{1,0:T(8,128)(2,1)S(1)}, bf16[512,1024]{1,0:T(8,128)(2,1)}, u32[]{:S(2)}) copy-start(bf16[512,1024]{1,0:T(8,128)(2,1)} %constant.17.clone.backward_ref) | copy-start | bytes 3145732
  18.9 1.5 %copy-start.2 = (bf16[4,256,256]{2,1,0:T(8,128)(2,1)S(1)}, bf16[4,256,256]{2,1,0:T(8,128)(2,1)}, u32[]{:S(2)}) copy-start(bf16[4,256,256]{2,1,0:T(8,128)(2,1)} %constant.15.clone.inverse_ref) | copy-start | bytes 1572868

commit v6 on v5

--- a/solution.py
+++ b/solution.py
@@ -185,12 +185,12 @@
     return jnp.concatenate([jnp.concatenate([re, im], axis=1), jnp.concatenate([im, -re], axis=1)], axis=0)
 
 
-def pack_kernel(signal_ref, real_ref, imag_ref, skip_ref, send_ref, skips_ref, signal_buf, sems):
+def pack_kernel(signal_ref, real_ref, imag_ref, skip_ref, send_ref, skips_ref, kept_ref, sems):
     _, parts, _, _ = send_ref.shape
     row_count = signal_ref.shape[-2]
     half = row_count // 2
     height = row_count // parts
-    copies = [(signal_ref, signal_buf), (skip_ref, skips_ref)]
+    copies = [(signal_ref, kept_ref), (skip_ref, skips_ref)]
     for part in range(parts):
         group = row_group(part // 2, part % 2, parts)
         cut = slice(group * height, (group + 1) * height)
@@ -200,7 +200,7 @@
     for copy in copies:
         copy.start()
     copies[0].wait()
-    halves = crossed(signal_buf[:, :half], signal_buf[:, half:])
+    halves = crossed(kept_ref[:, :half], kept_ref[:, half:])
     for part in range(parts):
         send_ref[:, part, :half] = halves[part % 2]
     for copy in copies[1:]:
@@ -220,8 +220,8 @@
     return jnp.concatenate([forward_ref[rows, :second_len], forward_ref[rows, second_len:]], axis=0)
 
 
-def near_kernel(got_ref, first_ref, block_ref, row_ref, forward_ref, skip_ref, spec_ref, twist_ref, term_ref, *, turn):
-    rows, parts, tall, width = got_ref.shape
+def near_kernel(got_ref, first_ref, block_ref, row_ref, forward_ref, spec_ref, twist_ref):
+    tall = got_ref.shape[2]
     side, core = side_and_core()
     first_len, second_len = first_ref.shape[-1], forward_ref.shape[0]
     height = tall // 4
@@ -232,16 +232,8 @@
     twist_ref[0], twist_ref[1] = twists(block_ref, row_ref, height, side, core, half_of(1 - core, near_len))
     twist_ref[2], twist_ref[3] = (each / (first_len * second_len) for each in twist)
 
-    at = lax.broadcasted_iota(jnp.int32, skip_ref.shape, 1)
-    channel = turn * rows + lax.axis_index("row")
-    skip = jnp.sum(jnp.where(at == channel, skip_ref[...], 0.0), axis=1, keepdims=True)
-    series = series_of(got_ref)
-    for place in range(parts // 2):
-        cut = slice(place * width, (place + 1) * width)
-        term_ref[:, cut] = jnp.where(side == place, skip, 0.0) * series[:, cut].astype(jnp.float32)
-
-
-def spectrum_kernel(spec_ref, twist_ref, term_ref, got_ref, swapped_ref, first_ref, forward_ref, backward_ref, inverse_ref, out_ref):
+
+def spectrum_kernel(spec_ref, twist_ref, got_ref, swapped_ref, first_ref, forward_ref, backward_ref, inverse_ref, out_ref):
     rows, parts, tall, width = got_ref.shape
     side, core = side_and_core()
     half, height = tall // 2, tall // 4
@@ -259,19 +251,23 @@
     back = dot(widened_back(prod), jnp.concatenate([backward_ref[:, col] for col in cols], axis=0))
     unwound = turned(back[:mine], back[mine:], twist_ref[2], -twist_ref[3])
     unwound = jnp.concatenate(unwound, axis=0).astype(jnp.bfloat16)
-    total = (dot(inverse_ref[lax.axis_index("col")], unwound) + term_ref[...]).astype(jnp.bfloat16)
+    total = dot(inverse_ref[lax.axis_index("col")], unwound).astype(jnp.bfloat16)
     for place in range(parts // 2):
         piece = total[:, place * width : (place + 1) * width].reshape(rows, 2 * half, width)
         out_ref[:, 2 * place], out_ref[:, 2 * place + 1] = crossed(piece[:, :half], piece[:, half:])
 
 
-def finish_kernel(back_ref, out_ref):
-    _, parts, half, _ = back_ref.shape
+def finish_kernel(back_ref, kept_ref, skips_ref, out_ref, *, turn):
+    rows, parts, half, _ = back_ref.shape
     cores = []
     for core in range(2):
         shares = [back_ref[:, part].astype(jnp.float32) for part in range(core, parts, 2)]
         cores.append(sum(shares[1:], shares[0]))
-    out_ref[:, :half], out_ref[:, half:] = (each.astype(jnp.bfloat16) for each in crossed(*cores))
+    sums = jnp.concatenate(crossed(*cores), axis=1)
+    for channel in range(rows):
+        at = turn * rows + channel
+        term = skips_ref[:, at : at + 1] * kept_ref[channel].astype(jnp.float32)
+        out_ref[channel] = (sums[channel] + term).astype(jnp.bfloat16)
 
 
 PARAMS = pltpu.CompilerParams(vmem_limit_bytes=8 * 2**20)
@@ -309,28 +305,25 @@
         own = slice(turn * rows, (turn + 1) * rows)
         tall = half + 2 * (row_count // parts)
         args = (signal[own], filter_real[own], filter_imag[own], skip[None])
-        send, skips = pl.pallas_call(
+        send, skips, kept = pl.pallas_call(
             pack_kernel,
-            out_shape=[pltpu.VMEM((rows, parts, tall, col_count), jnp.bfloat16), pltpu.VMEM((1, channels), jnp.float32)],
+            out_shape=[
+                pltpu.VMEM((rows, parts, tall, col_count), jnp.bfloat16),
+                pltpu.VMEM((1, channels), jnp.float32),
+                pltpu.VMEM((rows, row_count, col_count), jnp.bfloat16),
+            ],
             in_specs=[pl.BlockSpec(memory_space=pltpu.HBM)] * len(args),
-            out_specs=[IN_VMEM] * 2,
-            scratch_shapes=[
-                pltpu.VMEM((rows, row_count, col_count), jnp.bfloat16),
-                pltpu.SemaphoreType.DMA((2 * parts + 2,)),
-            ],
+            out_specs=[IN_VMEM] * 3,
+            scratch_shapes=[pltpu.SemaphoreType.DMA((2 * parts + 2,))],
             compiler_params=PARAMS,
             cost_estimate=pl.CostEstimate(flops=10**9, bytes_accessed=0, transcendentals=0),
         )(*(pltpu.with_memory_space_constraint(arg, pltpu.HBM) for arg in args))
         got = exchange(send)
         swapped = lax.ppermute(got, "col", pairs)
         near = call(
-            functools.partial(near_kernel, turn=turn),
-            [
-                ((2 * mine, 2 * near_len), jnp.float32),
-                ((4, mine, near_len), jnp.float32),
-                ((rows * row_count, near_len), jnp.float32),
-            ],
-            *(got, first, block, row, forward, skips),
+            near_kernel,
+            [((2 * mine, 2 * near_len), jnp.float32), ((4, mine, near_len), jnp.float32)],
+            *(got, first, block, row, forward),
             flops=10**9,
         )
         (partial_sums,) = call(
@@ -341,11 +334,11 @@
         back = exchange(partial_sums)
         outs.append(
             pl.pallas_call(
-                finish_kernel,
+                functools.partial(finish_kernel, turn=turn),
                 out_shape=jax.ShapeDtypeStruct((rows, row_count, col_count), jnp.bfloat16),
-                in_specs=[IN_VMEM],
+                in_specs=[IN_VMEM] * 3,
                 compiler_params=PARAMS,
-            )(pltpu.with_memory_space_constraint(back, pltpu.VMEM))
+            )(*(pltpu.with_memory_space_constraint(arg, pltpu.VMEM) for arg in (back, kept, skips)))
         )
     return outs[0] if share == 1 else jnp.concatenate(outs, axis=0)
 

time: 32.9 us -> 32.9 us (level)
  no operation moved by 1% of the time
where the time goes in v6:
time: 32.9 us; the launch traced here: 32.8 us
  blocking collectives  28.1 us (85%)
  Pallas kernels  3.56 us (11%)
  waiting for transfers between devices  0.98 us (3%)
    all_to_all x2, blocking collectives, exchange(): lax.all_to_all(flat, ('row', 'col'), 0, 0, tiled=True).reshape(array.shape)  28.1 us
    pallas_call x2, Pallas kernels, call(): pl.pallas_call(kernel, out_shape=[pltpu.VMEM(shape, kind) for shape, kind...  1.7 us
    pallas_call x1, Pallas kernels, local_by_channels(): pl.pallas_call(pack_kernel, out_shape=[pltpu.VMEM((rows, parts, tall, col...  1.12 us
    ppermute x1, waiting for transfers between devices, local_by_channels(): swapped = lax.ppermute(got, 'col', pairs)  0.98 us
    pallas_call x1, Pallas kernels, local_by_channels(): pl.pallas_call(functools.partial(finish_kernel, turn=turn), out_shape=jax...  0.75 us
  transfers between devices with their start and end apart: 1, of which 1 were waited for; matrix products, arithmetic and copies ran while one was open for 0% of the time, Pallas kernels for 2%

profile of v6, /device:TPU:0, one launch (start us, length us, event | category | flops | bytes accessed | tf_op | source)
XLA Modules:
  0.0 32.8 jit_solution(16617640315168965065)
XLA Ops:
  0.0 0.0 copy-start
  0.0 1.1 %shard_map.100 = (bf16[8,4,32,128]{3,2,1,0:T(8,128)(2,1)S(1)}, f32[1,8]{1,0:T(1,128)S(1)}, bf16[8,32,128]{2,1,0:T(8,128)(2,1)S(1)}) custom-call(bf16[8,32,128]{2,1,0:T(8,128)(2,1)} %signal_ref.1, bf16[8,32,128]{2,1,0:T(8,128)(2,1)} %real_ref.1, bf16[8,32,128]{2,1,0:T(8,128)(2,1)} %imag_ref.1, f32[1,8]{1,0:T(1,128)} %bitcast.11), custom_call_target="tpu_custom_call" | custom-call | flops 1000000000 | tf_op jit(solution)/shard_map/pallas_call | solution.py:308
  1.1 0.0 copy-start.3
  1.1 0.0 copy-start.4
  1.2 0.0 copy-start.5
  1.2 17.7 %all_to_all.10 = bf16[32,32,128]{2,1,0:T(8,128)(2,1)S(1)} all-to-all(bf16[32,32,128]{2,1,0:T(8,128)(2,1)S(1)} %bitcast.10), channel_id=1, replica_groups=mesh['row'=8,'col'=4] {'row','col'}, dimensions={0} | all-to-all | bytes 524288 | tf_op jit(solution)/shard_map/all_to_all | solution.py:302
  18.9 0.0 copy-start.1
  18.9 0.0 copy-start.2
  18.9 0.0 collective-permute-start
  18.9 0.0 copy-done
  18.9 0.0 copy-done.3
  18.9 0.0 copy-done.4
  18.9 0.0 copy-done.5
  18.9 0.5 %shard_map.101 = (f32[256,512]{1,0:T(8,128)S(1)}, f32[4,128,256]{2,1,0:T(8,128)S(1)}) custom-call(bf16[8,4,32,128]{3,2,1,0:T(8,128)(2,1)S(1)} %bitcast.6, bf16[2,2,2,64,256]{4,3,2,1,0:T(8,128)(2,1)S(1)} %copy-done.3, f32[2,8,512]{2,1,0:T(8,128)S(1)} %copy-done.5, f32[2,32,512]{2,1,0:T(8,128)S(1)} %copy-done.4, bf16[512,1024]{1,0:T(8,128)(2,1)S(1)} %copy-done), custom_call_target="tpu_custom_call" | custom-call | flops 1000000000 | tf_op jit(solution)/shard_map/pallas_call | solution.py:278
  19.4 1.0 %collective-permute-done.swapped_ref = bf16[8,4,32,128]{3,2,1,0:T(8,128)(2,1)S(1)} collective-permute-done((bf16[8,4,32,128]{3,2,1,0:T(8,128)(2,1)S(1)}, bf16[8,4,32,128]{3,2,1,0:T(8,128)(2,1)S(1)}, u32[]{:S(2)}, u32[]{:S(2)}) %collective-permute-start) | collective-permute-done | bytes 262176 | tf_op jit(solution)/shard_map/ppermute | solution.py:322
  20.4 0.0 copy-done.1
  20.4 0.0 copy-done.2
  20.4 1.2 %shard_map.102 = bf16[8,4,16,128]{3,2,1,0:T(8,128)(2,1)S(1)} custom-call(f32[256,512]{1,0:T(8,128)S(1)} %get-tuple-element.11.spec_ref, f32[4,128,256]{2,1,0:T(8,128)S(1)} %get-tuple-element.12.twist_ref, bf16[8,4,32,128]{3,2,1,0:T(8,128)(2,1)S(1)} %bitcast.7, bf16[8,4,32,128]{3,2,1,0:T(8,128)(2,1)S(1)} %collective-permute-done.swapped_ref, ...), custom_call_target="tpu_custom_call" | custom-call | tf_op jit(solution)/shard_map/pallas_call | solution.py:278
  21.6 10.4 %all_to_all.11 = bf16[32,16,128]{2,1,0:T(8,128)(2,1)S(1)} all-to-all(bf16[32,16,128]{2,1,0:T(8,128)(2,1)S(1)} %bitcast.8), channel_id=1, replica_groups=mesh['row'=8,'col'=4] {'row','col'}, dimensions={0} | all-to-all | bytes 262144 | tf_op jit(solution)/shard_map/all_to_all | solution.py:302
  32.0 0.7 %shard_map.103 = bf16[8,32,128]{2,1,0:T(8,128)(2,1)} custom-call(bf16[8,4,16,128]{3,2,1,0:T(8,128)(2,1)S(1)} %bitcast.9, bf16[8,32,128]{2,1,0:T(8,128)(2,1)S(1)} %get-tuple-element.13.kept_ref, f32[1,8]{1,0:T(1,128)S(1)} %get-tuple-element.14.skips_ref), custom_call_target="tpu_custom_call" | custom-call | tf_op jit(solution)/shard_map/pallas_call | solution.py:336
Async XLA Ops:
  0.0 18.9 %copy-start = (bf16[512,1024]{1,0:T(8,128)(2,1)S(1)}, bf16[512,1024]{1,0:T(8,128)(2,1)}, u32[]{:S(2)}) copy-start(bf16[512,1024]{1,0:T(8,128)(2,1)} %constant.16.clone.forward_ref) | copy-start | bytes 3145732
  1.1 17.8 %copy-start.3 = (bf16[2,2,2,64,256]{4,3,2,1,0:T(8,128)(2,1)S(1)}, bf16[2,2,2,64,256]{4,3,2,1,0:T(8,128)(2,1)}, u32[]{:S(2)}) copy-start(bf16[2,2,2,64,256]{4,3,2,1,0:T(8,128)(2,1)} %constant.12.clone.first_ref) | copy-start | bytes 786436
  1.1 17.8 %copy-start.4 = (f32[2,32,512]{2,1,0:T(8,128)S(1)}, f32[2,32,512]{2,1,0:T(8,128)}, u32[]{:S(2)}) copy-start(f32[2,32,512]{2,1,0:T(8,128)} %constant.14.clone.row_ref) | copy-start | bytes 393220
  1.2 17.8 %copy-start.5 = (f32[2,8,512]{2,1,0:T(8,128)S(1)}, f32[2,8,512]{2,1,0:T(8,128)}, u32[]{:S(2)}) copy-start(f32[2,8,512]{2,1,0:T(8,128)} %constant.13.clone.block_ref) | copy-start | bytes 98308
  18.9 1.5 %copy-start.1 = (bf16[512,1024]{1,0:T(8,128)(2,1)S(1)}, bf16[512,1024]{1,0:T(8,128)(2,1)}, u32[]{:S(2)}) copy-start(bf16[512,1024]{1,0:T(8,128)(2,1)} %constant.17.clone.backward_ref) | copy-start | bytes 3145732
  18.9 1.5 %copy-start.2 = (bf16[4,256,256]{2,1,0:T(8,128)(2,1)S(1)}, bf16[4,256,256]{2,1,0:T(8,128)(2,1)}, u32[]{:S(2)}) copy-start(bf16[4,256,256]{2,1,0:T(8,128)(2,1)} %constant.15.clone.inverse_ref) | copy-start | bytes 1572868
  18.9 1.5 %collective-permute-start = (bf16[8,4,32,128]{3,2,1,0:T(8,128)(2,1)S(1)}, bf16[8,4,32,128]{3,2,1,0:T(8,128)(2,1)S(1)}, u32[]{:S(2)}, u32[]{:S(2)}) collective-permute-start(bf16[8,4,32,128]{3,2,1,0:T(8,128)(2,1)S(1)} %bitcast.5), channel_id=1, source_target_pairs={{0,1},{1,0},{2,3},{3,2},{4,5},{5,4},{6,7},{7,6},{8,9},{9,8},{10,11... | collective-permute-start | bytes 786440 | tf_op jit(solution)/shard_map/ppermute | solution.py:322

commit v7 on v6

--- a/solution.py
+++ b/solution.py
@@ -131,6 +131,16 @@
     )
 
 
+def in_left(array):
+    axis = array.ndim - 1
+    return lax.broadcasted_iota(jnp.int32, array.shape, axis) < array.shape[axis] // 2
+
+
+def turned_over(array):
+    half = array.shape[-1] // 2
+    return jnp.concatenate([array[..., half:], array[..., :half]], axis=-1)
+
+
 def side_and_core():
     part = lax.axis_index("col")
     return part // 2, part % 2
@@ -145,7 +155,9 @@
     half = tall // 2
     strips = []
     for part in range(0, parts, 2):
-        pair = crossed(ref[:, part, :half, :], ref[:, part + 1, :half, :])
+        even, odd = ref[:, part, :half, :], ref[:, part + 1, :half, :]
+        left = in_left(even)
+        pair = [jnp.where(left, even, odd), turned_over(jnp.where(left, odd, even))]
         strips.append(jnp.concatenate(pair, axis=1).reshape(rows * 2 * half, width))
     return jnp.concatenate(strips, axis=1)
 
@@ -200,7 +212,9 @@
     for copy in copies:
         copy.start()
     copies[0].wait()
-    halves = crossed(kept_ref[:, :half], kept_ref[:, half:])
+    is_even = side_and_core()[1] == 0
+    upper, lower = kept_ref[:, :half], kept_ref[:, half:]
+    halves = crossed(jnp.where(is_even, upper, lower), jnp.where(is_even, lower, upper))
     for part in range(parts):
         send_ref[:, part, :half] = halves[part % 2]
     for copy in copies[1:]:
@@ -254,7 +268,10 @@
     total = dot(inverse_ref[lax.axis_index("col")], unwound).astype(jnp.bfloat16)
     for place in range(parts // 2):
         piece = total[:, place * width : (place + 1) * width].reshape(rows, 2 * half, width)
-        out_ref[:, 2 * place], out_ref[:, 2 * place + 1] = crossed(piece[:, :half], piece[:, half:])
+        upper, lower = piece[:, :half], turned_over(piece[:, half:])
+        left = in_left(upper)
+        out_ref[:, 2 * place] = jnp.where(left, upper, lower)
+        out_ref[:, 2 * place + 1] = jnp.where(left, lower, upper)
 
 
 def finish_kernel(back_ref, kept_ref, skips_ref, out_ref, *, turn):
@@ -263,7 +280,9 @@
     for core in range(2):
         shares = [back_ref[:, part].astype(jnp.float32) for part in range(core, parts, 2)]
         cores.append(sum(shares[1:], shares[0]))
-    sums = jnp.concatenate(crossed(*cores), axis=1)
+    one, two = crossed(*cores)
+    is_even = side_and_core()[1] == 0
+    sums = jnp.concatenate([jnp.where(is_even, one, two), jnp.where(is_even, two, one)], axis=1)
     for channel in range(rows):
         at = turn * rows + channel
         term = skips_ref[:, at : at + 1] * kept_ref[channel].astype(jnp.float32)

time: 32.9 us -> 33 us (level)
  no operation moved by 1% of the time
where the time goes in v7:
time: 33 us; the launch traced here: 32.8 us
  blocking collectives  28.1 us (85%)
  Pallas kernels  3.57 us (11%)
  waiting for transfers between devices  0.98 us (3%)
    all_to_all x2, blocking collectives, exchange(): lax.all_to_all(flat, ('row', 'col'), 0, 0, tiled=True).reshape(array.shape)  28.1 us
    pallas_call x2, Pallas kernels, call(): pl.pallas_call(kernel, out_shape=[pltpu.VMEM(shape, kind) for shape, kind...  1.69 us
    pallas_call x1, Pallas kernels, local_by_channels(): pl.pallas_call(pack_kernel, out_shape=[pltpu.VMEM((rows, parts, tall, col...  1.13 us
    ppermute x1, waiting for transfers between devices, local_by_channels(): swapped = lax.ppermute(got, 'col', pairs)  0.98 us
    pallas_call x1, Pallas kernels, local_by_channels(): pl.pallas_call(functools.partial(finish_kernel, turn=turn), out_shape=jax...  0.75 us
  transfers between devices with their start and end apart: 1, of which 1 were waited for; matrix products, arithmetic and copies ran while one was open for 0% of the time, Pallas kernels for 2%

profile of v7, /device:TPU:0, one launch (start us, length us, event | category | flops | bytes accessed | tf_op | source)
XLA Modules:
  0.0 32.8 jit_solution(4495647241605796107)
XLA Ops:
  0.0 0.0 copy-start
  0.0 1.1 %shard_map.100 = (bf16[8,4,32,128]{3,2,1,0:T(8,128)(2,1)S(1)}, f32[1,8]{1,0:T(1,128)S(1)}, bf16[8,32,128]{2,1,0:T(8,128)(2,1)S(1)}) custom-call(bf16[8,32,128]{2,1,0:T(8,128)(2,1)} %signal_ref.1, bf16[8,32,128]{2,1,0:T(8,128)(2,1)} %real_ref.1, bf16[8,32,128]{2,1,0:T(8,128)(2,1)} %imag_ref.1, f32[1,8]{1,0:T(1,128)} %bitcast.11), custom_call_target="tpu_custom_call" | custom-call | flops 1000000000 | tf_op jit(solution)/shard_map/pallas_call | solution.py:327
  1.1 0.0 copy-start.3
  1.1 0.0 copy-start.4
  1.2 0.0 copy-start.5
  1.2 17.7 %all_to_all.10 = bf16[32,32,128]{2,1,0:T(8,128)(2,1)S(1)} all-to-all(bf16[32,32,128]{2,1,0:T(8,128)(2,1)S(1)} %bitcast.10), channel_id=1, replica_groups=mesh['row'=8,'col'=4] {'row','col'}, dimensions={0} | all-to-all | bytes 524288 | tf_op jit(solution)/shard_map/all_to_all | solution.py:321
  18.9 0.0 copy-start.1
  18.9 0.0 copy-start.2
  18.9 0.0 collective-permute-start
  18.9 0.0 copy-done
  18.9 0.0 copy-done.3
  18.9 0.0 copy-done.4
  18.9 0.0 copy-done.5
  18.9 0.5 %shard_map.101 = (f32[256,512]{1,0:T(8,128)S(1)}, f32[4,128,256]{2,1,0:T(8,128)S(1)}) custom-call(bf16[8,4,32,128]{3,2,1,0:T(8,128)(2,1)S(1)} %bitcast.6, bf16[2,2,2,64,256]{4,3,2,1,0:T(8,128)(2,1)S(1)} %copy-done.3, f32[2,8,512]{2,1,0:T(8,128)S(1)} %copy-done.5, f32[2,32,512]{2,1,0:T(8,128)S(1)} %copy-done.4, bf16[512,1024]{1,0:T(8,128)(2,1)S(1)} %copy-done), custom_call_target="tpu_custom_call" | custom-call | flops 1000000000 | tf_op jit(solution)/shard_map/pallas_call | solution.py:297
  19.4 1.0 %collective-permute-done.swapped_ref = bf16[8,4,32,128]{3,2,1,0:T(8,128)(2,1)S(1)} collective-permute-done((bf16[8,4,32,128]{3,2,1,0:T(8,128)(2,1)S(1)}, bf16[8,4,32,128]{3,2,1,0:T(8,128)(2,1)S(1)}, u32[]{:S(2)}, u32[]{:S(2)}) %collective-permute-start) | collective-permute-done | bytes 262176 | tf_op jit(solution)/shard_map/ppermute | solution.py:341
  20.4 0.0 copy-done.1
  20.4 0.0 copy-done.2
  20.4 1.2 %shard_map.102 = bf16[8,4,16,128]{3,2,1,0:T(8,128)(2,1)S(1)} custom-call(f32[256,512]{1,0:T(8,128)S(1)} %get-tuple-element.11.spec_ref, f32[4,128,256]{2,1,0:T(8,128)S(1)} %get-tuple-element.12.twist_ref, bf16[8,4,32,128]{3,2,1,0:T(8,128)(2,1)S(1)} %bitcast.7, bf16[8,4,32,128]{3,2,1,0:T(8,128)(2,1)S(1)} %collective-permute-done.swapped_ref, ...), custom_call_target="tpu_custom_call" | custom-call | tf_op jit(solution)/shard_map/pallas_call | solution.py:297
  21.6 10.4 %all_to_all.11 = bf16[32,16,128]{2,1,0:T(8,128)(2,1)S(1)} all-to-all(bf16[32,16,128]{2,1,0:T(8,128)(2,1)S(1)} %bitcast.8), channel_id=1, replica_groups=mesh['row'=8,'col'=4] {'row','col'}, dimensions={0} | all-to-all | bytes 262144 | tf_op jit(solution)/shard_map/all_to_all | solution.py:321
  32.0 0.8 %shard_map.103 = bf16[8,32,128]{2,1,0:T(8,128)(2,1)} custom-call(bf16[8,4,16,128]{3,2,1,0:T(8,128)(2,1)S(1)} %bitcast.9, bf16[8,32,128]{2,1,0:T(8,128)(2,1)S(1)} %get-tuple-element.13.kept_ref, f32[1,8]{1,0:T(1,128)S(1)} %get-tuple-element.14.skips_ref), custom_call_target="tpu_custom_call" | custom-call | tf_op jit(solution)/shard_map/pallas_call | solution.py:355
Async XLA Ops:
  0.0 18.9 %copy-start = (bf16[512,1024]{1,0:T(8,128)(2,1)S(1)}, bf16[512,1024]{1,0:T(8,128)(2,1)}, u32[]{:S(2)}) copy-start(bf16[512,1024]{1,0:T(8,128)(2,1)} %constant.16.clone.forward_ref) | copy-start | bytes 3145732
  1.1 17.8 %copy-start.3 = (bf16[2,2,2,64,256]{4,3,2,1,0:T(8,128)(2,1)S(1)}, bf16[2,2,2,64,256]{4,3,2,1,0:T(8,128)(2,1)}, u32[]{:S(2)}) copy-start(bf16[2,2,2,64,256]{4,3,2,1,0:T(8,128)(2,1)} %constant.12.clone.first_ref) | copy-start | bytes 786436
  1.1 17.8 %copy-start.4 = (f32[2,32,512]{2,1,0:T(8,128)S(1)}, f32[2,32,512]{2,1,0:T(8,128)}, u32[]{:S(2)}) copy-start(f32[2,32,512]{2,1,0:T(8,128)} %constant.14.clone.row_ref) | copy-start | bytes 393220
  1.2 17.8 %copy-start.5 = (f32[2,8,512]{2,1,0:T(8,128)S(1)}, f32[2,8,512]{2,1,0:T(8,128)}, u32[]{:S(2)}) copy-start(f32[2,8,512]{2,1,0:T(8,128)} %constant.13.clone.block_ref) | copy-start | bytes 98308
  18.9 1.5 %copy-start.1 = (bf16[512,1024]{1,0:T(8,128)(2,1)S(1)}, bf16[512,1024]{1,0:T(8,128)(2,1)}, u32[]{:S(2)}) copy-start(bf16[512,1024]{1,0:T(8,128)(2,1)} %constant.17.clone.backward_ref) | copy-start | bytes 3145732
  18.9 1.5 %copy-start.2 = (bf16[4,256,256]{2,1,0:T(8,128)(2,1)S(1)}, bf16[4,256,256]{2,1,0:T(8,128)(2,1)}, u32[]{:S(2)}) copy-start(bf16[4,256,256]{2,1,0:T(8,128)(2,1)} %constant.15.clone.inverse_ref) | copy-start | bytes 1572868
  18.9 1.5 %collective-permute-start = (bf16[8,4,32,128]{3,2,1,0:T(8,128)(2,1)S(1)}, bf16[8,4,32,128]{3,2,1,0:T(8,128)(2,1)S(1)}, u32[]{:S(2)}, u32[]{:S(2)}) collective-permute-start(bf16[8,4,32,128]{3,2,1,0:T(8,128)(2,1)S(1)} %bitcast.5), channel_id=1, source_target_pairs={{0,1},{1,0},{2,3},{3,2},{4,5},{5,4},{6,7},{7,6},{8,9},{9,8},{10,11... | collective-permute-start | bytes 786440 | tf_op jit(solution)/shard_map/ppermute | solution.py:341

commit v8 on v6

--- a/solution.py
+++ b/solution.py
@@ -180,11 +180,6 @@
     return jnp.concatenate([jnp.concatenate([re, -im], axis=1), jnp.concatenate([im, re], axis=1)], axis=0)
 
 
-def widened_back(pair):
-    re, im = (each.astype(jnp.bfloat16) for each in pair)
-    return jnp.concatenate([jnp.concatenate([re, im], axis=1), jnp.concatenate([im, -re], axis=1)], axis=0)
-
-
 def pack_kernel(signal_ref, real_ref, imag_ref, skip_ref, send_ref, skips_ref, kept_ref, sems):
     _, parts, _, _ = send_ref.shape
     row_count = signal_ref.shape[-2]
@@ -248,8 +243,11 @@
     )
     prod = turned(spec[:mine], spec[mine:], filt_re, filt_im)
     cols = [pl.ds(pl.multiple_of(at + core * near_len, near_len), near_len) for at in (0, second_len)]
-    back = dot(widened_back(prod), jnp.concatenate([backward_ref[:, col] for col in cols], axis=0))
-    unwound = turned(back[:mine], back[mine:], twist_ref[2], -twist_ref[3])
+    prod = jnp.concatenate(prod, axis=0).astype(jnp.bfloat16)
+    both = dot(prod, jnp.concatenate([backward_ref[:, col] for col in cols], axis=1))
+    back_re = both[:mine, :near_len] + both[mine:, near_len:]
+    back_im = both[mine:, :near_len] - both[:mine, near_len:]
+    unwound = turned(back_re, back_im, twist_ref[2], -twist_ref[3])
     unwound = jnp.concatenate(unwound, axis=0).astype(jnp.bfloat16)
     total = dot(inverse_ref[lax.axis_index("col")], unwound).astype(jnp.bfloat16)
     for place in range(parts // 2):

time: 32.9 us -> 32.9 us (level)
  no operation moved by 1% of the time
where the time goes in v8:
time: 32.9 us; the launch traced here: 32.8 us
  blocking collectives  28.1 us (85%)
  Pallas kernels  3.57 us (11%)
  waiting for transfers between devices  0.98 us (3%)
    all_to_all x2, blocking collectives, exchange(): lax.all_to_all(flat, ('row', 'col'), 0, 0, tiled=True).reshape(array.shape)  28.1 us
    pallas_call x2, Pallas kernels, call(): pl.pallas_call(kernel, out_shape=[pltpu.VMEM(shape, kind) for shape, kind...  1.7 us
    pallas_call x1, Pallas kernels, local_by_channels(): pl.pallas_call(pack_kernel, out_shape=[pltpu.VMEM((rows, parts, tall, col...  1.12 us
    ppermute x1, waiting for transfers between devices, local_by_channels(): swapped = lax.ppermute(got, 'col', pairs)  0.98 us
    pallas_call x1, Pallas kernels, local_by_channels(): pl.pallas_call(functools.partial(finish_kernel, turn=turn), out_shape=jax...  0.75 us
  transfers between devices with their start and end apart: 1, of which 1 were waited for; matrix products, arithmetic and copies ran while one was open for 0% of the time, Pallas kernels for 2%

profile of v8, /device:TPU:0, one launch (start us, length us, event | category | flops | bytes accessed | tf_op | source)
XLA Modules:
  0.0 32.8 jit_solution(5370240030482059147)
XLA Ops:
  0.0 0.0 copy-start
  0.0 1.1 %shard_map.100 = (bf16[8,4,32,128]{3,2,1,0:T(8,128)(2,1)S(1)}, f32[1,8]{1,0:T(1,128)S(1)}, bf16[8,32,128]{2,1,0:T(8,128)(2,1)S(1)}) custom-call(bf16[8,32,128]{2,1,0:T(8,128)(2,1)} %signal_ref.1, bf16[8,32,128]{2,1,0:T(8,128)(2,1)} %real_ref.1, bf16[8,32,128]{2,1,0:T(8,128)(2,1)} %imag_ref.1, f32[1,8]{1,0:T(1,128)} %bitcast.11), custom_call_target="tpu_custom_call" | custom-call | flops 1000000000 | tf_op jit(solution)/shard_map/pallas_call | solution.py:306
  1.1 0.0 copy-start.3
  1.1 0.0 copy-start.4
  1.2 0.0 copy-start.5
  1.2 17.7 %all_to_all.10 = bf16[32,32,128]{2,1,0:T(8,128)(2,1)S(1)} all-to-all(bf16[32,32,128]{2,1,0:T(8,128)(2,1)S(1)} %bitcast.10), channel_id=1, replica_groups=mesh['row'=8,'col'=4] {'row','col'}, dimensions={0} | all-to-all | bytes 524288 | tf_op jit(solution)/shard_map/all_to_all | solution.py:300
  18.9 0.0 copy-start.1
  18.9 0.0 copy-start.2
  18.9 0.0 collective-permute-start
  18.9 0.0 copy-done
  18.9 0.0 copy-done.3
  18.9 0.0 copy-done.4
  18.9 0.0 copy-done.5
  18.9 0.5 %shard_map.101 = (f32[256,512]{1,0:T(8,128)S(1)}, f32[4,128,256]{2,1,0:T(8,128)S(1)}) custom-call(bf16[8,4,32,128]{3,2,1,0:T(8,128)(2,1)S(1)} %bitcast.6, bf16[2,2,2,64,256]{4,3,2,1,0:T(8,128)(2,1)S(1)} %copy-done.3, f32[2,8,512]{2,1,0:T(8,128)S(1)} %copy-done.5, f32[2,32,512]{2,1,0:T(8,128)S(1)} %copy-done.4, bf16[512,1024]{1,0:T(8,128)(2,1)S(1)} %copy-done), custom_call_target="tpu_custom_call" | custom-call | flops 1000000000 | tf_op jit(solution)/shard_map/pallas_call | solution.py:276
  19.4 1.0 %collective-permute-done.swapped_ref = bf16[8,4,32,128]{3,2,1,0:T(8,128)(2,1)S(1)} collective-permute-done((bf16[8,4,32,128]{3,2,1,0:T(8,128)(2,1)S(1)}, bf16[8,4,32,128]{3,2,1,0:T(8,128)(2,1)S(1)}, u32[]{:S(2)}, u32[]{:S(2)}) %collective-permute-start) | collective-permute-done | bytes 262176 | tf_op jit(solution)/shard_map/ppermute | solution.py:320
  20.4 0.0 copy-done.1
  20.4 0.0 copy-done.2
  20.4 1.2 %shard_map.102 = bf16[8,4,16,128]{3,2,1,0:T(8,128)(2,1)S(1)} custom-call(f32[256,512]{1,0:T(8,128)S(1)} %get-tuple-element.11.spec_ref, f32[4,128,256]{2,1,0:T(8,128)S(1)} %get-tuple-element.12.twist_ref, bf16[8,4,32,128]{3,2,1,0:T(8,128)(2,1)S(1)} %bitcast.7, bf16[8,4,32,128]{3,2,1,0:T(8,128)(2,1)S(1)} %collective-permute-done.swapped_ref, ...), custom_call_target="tpu_custom_call" | custom-call | tf_op jit(solution)/shard_map/pallas_call | solution.py:276
  21.6 10.4 %all_to_all.11 = bf16[32,16,128]{2,1,0:T(8,128)(2,1)S(1)} all-to-all(bf16[32,16,128]{2,1,0:T(8,128)(2,1)S(1)} %bitcast.8), channel_id=1, replica_groups=mesh['row'=8,'col'=4] {'row','col'}, dimensions={0} | all-to-all | bytes 262144 | tf_op jit(solution)/shard_map/all_to_all | solution.py:300
  32.0 0.7 %shard_map.103 = bf16[8,32,128]{2,1,0:T(8,128)(2,1)} custom-call(bf16[8,4,16,128]{3,2,1,0:T(8,128)(2,1)S(1)} %bitcast.9, bf16[8,32,128]{2,1,0:T(8,128)(2,1)S(1)} %get-tuple-element.13.kept_ref, f32[1,8]{1,0:T(1,128)S(1)} %get-tuple-element.14.skips_ref), custom_call_target="tpu_custom_call" | custom-call | tf_op jit(solution)/shard_map/pallas_call | solution.py:334
Async XLA Ops:
  0.0 18.9 %copy-start = (bf16[512,1024]{1,0:T(8,128)(2,1)S(1)}, bf16[512,1024]{1,0:T(8,128)(2,1)}, u32[]{:S(2)}) copy-start(bf16[512,1024]{1,0:T(8,128)(2,1)} %constant.16.clone.forward_ref) | copy-start | bytes 3145732
  1.1 17.8 %copy-start.3 = (bf16[2,2,2,64,256]{4,3,2,1,0:T(8,128)(2,1)S(1)}, bf16[2,2,2,64,256]{4,3,2,1,0:T(8,128)(2,1)}, u32[]{:S(2)}) copy-start(bf16[2,2,2,64,256]{4,3,2,1,0:T(8,128)(2,1)} %constant.12.clone.first_ref) | copy-start | bytes 786436
  1.1 17.8 %copy-start.4 = (f32[2,32,512]{2,1,0:T(8,128)S(1)}, f32[2,32,512]{2,1,0:T(8,128)}, u32[]{:S(2)}) copy-start(f32[2,32,512]{2,1,0:T(8,128)} %constant.14.clone.row_ref) | copy-start | bytes 393220
  1.2 17.8 %copy-start.5 = (f32[2,8,512]{2,1,0:T(8,128)S(1)}, f32[2,8,512]{2,1,0:T(8,128)}, u32[]{:S(2)}) copy-start(f32[2,8,512]{2,1,0:T(8,128)} %constant.13.clone.block_ref) | copy-start | bytes 98308
  18.9 1.5 %copy-start.1 = (bf16[512,1024]{1,0:T(8,128)(2,1)S(1)}, bf16[512,1024]{1,0:T(8,128)(2,1)}, u32[]{:S(2)}) copy-start(bf16[512,1024]{1,0:T(8,128)(2,1)} %constant.17.clone.backward_ref) | copy-start | bytes 3145732
  18.9 1.5 %copy-start.2 = (bf16[4,256,256]{2,1,0:T(8,128)(2,1)S(1)}, bf16[4,256,256]{2,1,0:T(8,128)(2,1)}, u32[]{:S(2)}) copy-start(bf16[4,256,256]{2,1,0:T(8,128)(2,1)} %constant.15.clone.inverse_ref) | copy-start | bytes 1572868
  18.9 1.5 %collective-permute-start = (bf16[8,4,32,128]{3,2,1,0:T(8,128)(2,1)S(1)}, bf16[8,4,32,128]{3,2,1,0:T(8,128)(2,1)S(1)}, u32[]{:S(2)}, u32[]{:S(2)}) collective-permute-start(bf16[8,4,32,128]{3,2,1,0:T(8,128)(2,1)S(1)} %bitcast.5), channel_id=1, source_target_pairs={{0,1},{1,0},{2,3},{3,2},{4,5},{5,4},{6,7},{7,6},{8,9},{9,8},{10,11... | collective-permute-start | bytes 786440 | tf_op jit(solution)/shard_map/ppermute | solution.py:320

commit v9 on v7

--- a/solution.py
+++ b/solution.py
@@ -197,18 +197,13 @@
     return jnp.concatenate([jnp.concatenate([re, im], axis=1), jnp.concatenate([im, -re], axis=1)], axis=0)
 
 
-def pack_kernel(signal_ref, real_ref, imag_ref, skip_ref, send_ref, skips_ref, kept_ref, sems):
+def pack_kernel(signal_ref, real_ref, imag_ref, skip_ref, send_ref, skips_ref, kept_ref, real_buf, imag_buf, sems):
     _, parts, _, _ = send_ref.shape
     row_count = signal_ref.shape[-2]
     half = row_count // 2
     height = row_count // parts
-    copies = [(signal_ref, kept_ref), (skip_ref, skips_ref)]
-    for part in range(parts):
-        group = row_group(part // 2, part % 2, parts)
-        cut = slice(group * height, (group + 1) * height)
-        copies.append((real_ref.at[:, cut], send_ref.at[:, part, half : half + height]))
-        copies.append((imag_ref.at[:, cut], send_ref.at[:, part, half + height :]))
-    copies = [pltpu.make_async_copy(a, b, sems.at[i]) for i, (a, b) in enumerate(copies)]
+    moves = ((signal_ref, kept_ref), (real_ref, real_buf), (imag_ref, imag_buf), (skip_ref, skips_ref))
+    copies = [pltpu.make_async_copy(a, b, sems.at[i]) for i, (a, b) in enumerate(moves)]
     for copy in copies:
         copy.start()
     copies[0].wait()
@@ -217,8 +212,12 @@
     halves = crossed(jnp.where(is_even, upper, lower), jnp.where(is_even, lower, upper))
     for part in range(parts):
         send_ref[:, part, :half] = halves[part % 2]
-    for copy in copies[1:]:
+    for buf, copy, start in ((real_buf, copies[1], half), (imag_buf, copies[2], half + height)):
         copy.wait()
+        for part in range(parts):
+            group = row_group(part // 2, part % 2, parts)
+            send_ref[:, part, start : start + height] = buf[:, group * height : (group + 1) * height]
+    copies[3].wait()
 
 
 def half_transform(ref, first_ref, side, core):
@@ -333,7 +332,10 @@
             ],
             in_specs=[pl.BlockSpec(memory_space=pltpu.HBM)] * len(args),
             out_specs=[IN_VMEM] * 3,
-            scratch_shapes=[pltpu.SemaphoreType.DMA((2 * parts + 2,))],
+            scratch_shapes=[
+                *[pltpu.VMEM((rows, row_count, col_count), jnp.bfloat16)] * 2,
+                pltpu.SemaphoreType.DMA((4,)),
+            ],
             compiler_params=PARAMS,
             cost_estimate=pl.CostEstimate(flops=10**9, bytes_accessed=0, transcendentals=0),
         )(*(pltpu.with_memory_space_constraint(arg, pltpu.HBM) for arg in args))

time: 33 us -> 32.9 us (level)
  no operation moved by 1% of the time
where the time goes in v9:
time: 32.9 us; the launch traced here: 32.7 us
  blocking collectives  28.1 us (85%)
  Pallas kernels  3.54 us (11%)
  waiting for transfers between devices  0.98 us (3%)
    all_to_all x2, blocking collectives, exchange(): lax.all_to_all(flat, ('row', 'col'), 0, 0, tiled=True).reshape(array.shape)  28.1 us
    pallas_call x2, Pallas kernels, call(): pl.pallas_call(kernel, out_shape=[pltpu.VMEM(shape, kind) for shape, kind...  1.7 us
    pallas_call x1, Pallas kernels, local_by_channels(): pl.pallas_call(pack_kernel, out_shape=[pltpu.VMEM((rows, parts, tall, col...  1.09 us
    ppermute x1, waiting for transfers between devices, local_by_channels(): swapped = lax.ppermute(got, 'col', pairs)  0.98 us
    pallas_call x1, Pallas kernels, local_by_channels(): pl.pallas_call(functools.partial(finish_kernel, turn=turn), out_shape=jax...  0.75 us
  transfers between devices with their start and end apart: 1, of which 1 were waited for; matrix products, arithmetic and copies ran while one was open for 0% of the time, Pallas kernels for 2%

profile of v9, /device:TPU:0, one launch (start us, length us, event | category | flops | bytes accessed | tf_op | source)
XLA Modules:
  0.0 32.7 jit_solution(8598260332265024945)
XLA Ops:
  0.0 0.0 copy-start
  0.0 1.1 %shard_map.100 = (bf16[8,4,32,128]{3,2,1,0:T(8,128)(2,1)S(1)}, f32[1,8]{1,0:T(1,128)S(1)}, bf16[8,32,128]{2,1,0:T(8,128)(2,1)S(1)}) custom-call(bf16[8,32,128]{2,1,0:T(8,128)(2,1)} %signal_ref.1, bf16[8,32,128]{2,1,0:T(8,128)(2,1)} %real_ref.1, bf16[8,32,128]{2,1,0:T(8,128)(2,1)} %imag_ref.1, f32[1,8]{1,0:T(1,128)} %bitcast.11), custom_call_target="tpu_custom_call" | custom-call | flops 1000000000 | tf_op jit(solution)/shard_map/pallas_call | solution.py:326
  1.1 0.0 copy-start.3
  1.1 0.0 copy-start.4
  1.1 0.0 copy-start.5
  1.1 17.7 %all_to_all.10 = bf16[32,32,128]{2,1,0:T(8,128)(2,1)S(1)} all-to-all(bf16[32,32,128]{2,1,0:T(8,128)(2,1)S(1)} %bitcast.10), channel_id=1, replica_groups=mesh['row'=8,'col'=4] {'row','col'}, dimensions={0} | all-to-all | bytes 524288 | tf_op jit(solution)/shard_map/all_to_all | solution.py:320
  18.8 0.0 copy-start.1
  18.8 0.0 copy-start.2
  18.8 0.0 collective-permute-start
  18.8 0.0 copy-done
  18.9 0.0 copy-done.3
  18.9 0.0 copy-done.4
  18.9 0.0 copy-done.5
  18.9 0.5 %shard_map.101 = (f32[256,512]{1,0:T(8,128)S(1)}, f32[4,128,256]{2,1,0:T(8,128)S(1)}) custom-call(bf16[8,4,32,128]{3,2,1,0:T(8,128)(2,1)S(1)} %bitcast.6, bf16[2,2,2,64,256]{4,3,2,1,0:T(8,128)(2,1)S(1)} %copy-done.3, f32[2,8,512]{2,1,0:T(8,128)S(1)} %copy-done.5, f32[2,32,512]{2,1,0:T(8,128)S(1)} %copy-done.4, bf16[512,1024]{1,0:T(8,128)(2,1)S(1)} %copy-done), custom_call_target="tpu_custom_call" | custom-call | flops 1000000000 | tf_op jit(solution)/shard_map/pallas_call | solution.py:296
  19.4 1.0 %collective-permute-done.swapped_ref = bf16[8,4,32,128]{3,2,1,0:T(8,128)(2,1)S(1)} collective-permute-done((bf16[8,4,32,128]{3,2,1,0:T(8,128)(2,1)S(1)}, bf16[8,4,32,128]{3,2,1,0:T(8,128)(2,1)S(1)}, u32[]{:S(2)}, u32[]{:S(2)}) %collective-permute-start) | collective-permute-done | bytes 262176 | tf_op jit(solution)/shard_map/ppermute | solution.py:343
  20.4 0.0 copy-done.1
  20.4 0.0 copy-done.2
  20.4 1.2 %shard_map.102 = bf16[8,4,16,128]{3,2,1,0:T(8,128)(2,1)S(1)} custom-call(f32[256,512]{1,0:T(8,128)S(1)} %get-tuple-element.11.spec_ref, f32[4,128,256]{2,1,0:T(8,128)S(1)} %get-tuple-element.12.twist_ref, bf16[8,4,32,128]{3,2,1,0:T(8,128)(2,1)S(1)} %bitcast.7, bf16[8,4,32,128]{3,2,1,0:T(8,128)(2,1)S(1)} %collective-permute-done.swapped_ref, ...), custom_call_target="tpu_custom_call" | custom-call | tf_op jit(solution)/shard_map/pallas_call | solution.py:296
  21.6 10.4 %all_to_all.11 = bf16[32,16,128]{2,1,0:T(8,128)(2,1)S(1)} all-to-all(bf16[32,16,128]{2,1,0:T(8,128)(2,1)S(1)} %bitcast.8), channel_id=1, replica_groups=mesh['row'=8,'col'=4] {'row','col'}, dimensions={0} | all-to-all | bytes 262144 | tf_op jit(solution)/shard_map/all_to_all | solution.py:320
  32.0 0.8 %shard_map.103 = bf16[8,32,128]{2,1,0:T(8,128)(2,1)} custom-call(bf16[8,4,16,128]{3,2,1,0:T(8,128)(2,1)S(1)} %bitcast.9, bf16[8,32,128]{2,1,0:T(8,128)(2,1)S(1)} %get-tuple-element.13.kept_ref, f32[1,8]{1,0:T(1,128)S(1)} %get-tuple-element.14.skips_ref), custom_call_target="tpu_custom_call" | custom-call | tf_op jit(solution)/shard_map/pallas_call | solution.py:357
Async XLA Ops:
  0.0 18.9 %copy-start = (bf16[512,1024]{1,0:T(8,128)(2,1)S(1)}, bf16[512,1024]{1,0:T(8,128)(2,1)}, u32[]{:S(2)}) copy-start(bf16[512,1024]{1,0:T(8,128)(2,1)} %constant.16.clone.forward_ref) | copy-start | bytes 3145732
  1.1 17.8 %copy-start.3 = (bf16[2,2,2,64,256]{4,3,2,1,0:T(8,128)(2,1)S(1)}, bf16[2,2,2,64,256]{4,3,2,1,0:T(8,128)(2,1)}, u32[]{:S(2)}) copy-start(bf16[2,2,2,64,256]{4,3,2,1,0:T(8,128)(2,1)} %constant.12.clone.first_ref) | copy-start | bytes 786436
  1.1 17.8 %copy-start.4 = (f32[2,32,512]{2,1,0:T(8,128)S(1)}, f32[2,32,512]{2,1,0:T(8,128)}, u32[]{:S(2)}) copy-start(f32[2,32,512]{2,1,0:T(8,128)} %constant.14.clone.row_ref) | copy-start | bytes 393220
  1.1 17.8 %copy-start.5 = (f32[2,8,512]{2,1,0:T(8,128)S(1)}, f32[2,8,512]{2,1,0:T(8,128)}, u32[]{:S(2)}) copy-start(f32[2,8,512]{2,1,0:T(8,128)} %constant.13.clone.block_ref) | copy-start | bytes 98308
  18.8 1.5 %copy-start.1 = (bf16[512,1024]{1,0:T(8,128)(2,1)S(1)}, bf16[512,1024]{1,0:T(8,128)(2,1)}, u32[]{:S(2)}) copy-start(bf16[512,1024]{1,0:T(8,128)(2,1)} %constant.17.clone.backward_ref) | copy-start | bytes 3145732
  18.8 1.5 %copy-start.2 = (bf16[4,256,256]{2,1,0:T(8,128)(2,1)S(1)}, bf16[4,256,256]{2,1,0:T(8,128)(2,1)}, u32[]{:S(2)}) copy-start(bf16[4,256,256]{2,1,0:T(8,128)(2,1)} %constant.15.clone.inverse_ref) | copy-start | bytes 1572868
  18.8 1.5 %collective-permute-start = (bf16[8,4,32,128]{3,2,1,0:T(8,128)(2,1)S(1)}, bf16[8,4,32,128]{3,2,1,0:T(8,128)(2,1)S(1)}, u32[]{:S(2)}, u32[]{:S(2)}) collective-permute-start(bf16[8,4,32,128]{3,2,1,0:T(8,128)(2,1)S(1)} %bitcast.5), channel_id=1, source_target_pairs={{0,1},{1,0},{2,3},{3,2},{4,5},{5,4},{6,7},{7,6},{8,9},{9,8},{10,11... | collective-permute-start | bytes 786440 | tf_op jit(solution)/shard_map/ppermute | solution.py:343
